TPU v7x, 128 devices: a whole 4x4x4 slice. The times are simulated.
128 devices in a mesh: fsdp: 16 (over z, y), tensor: 8 (over x, core).
Axes of the slice: x: 4, y: 4, z: 4, core: 2. Of those that a mesh axis runs over, the one named last changes fastest.
Arguments:
- grad_blocks: bfloat16 [2, 16896, 1536], P(None, 'tensor', 'fsdp'), may hold values from -150 to 150
- master_shard: float32 [2, 16896, 1536], P(None, ('fsdp', 'tensor')), may hold values from -6 to 6
- first_moment: float32 [2, 16896, 1536], P(None, ('fsdp', 'tensor')), may hold values from -2 to 2
- second_moment: float32 [2, 16896, 1536], P(None, ('fsdp', 'tensor')), may hold values from 0.05 to 0.5
- average_shard: float32 [2, 16896, 1536], P(None, ('tensor', 'fsdp')), may hold values from -6 to 6
- gain_grads: bfloat16 [2, 3072], P(None, ('fsdp', 'tensor')), may hold values from -24 to 24
- gain_master: float32 [2, 3072], P(None, ('fsdp', 'tensor')), may hold values from 0.5 to 1.5
- gain_first: float32 [2, 3072], P(None, ('fsdp', 'tensor')), may hold values from -2 to 2
- gain_second: float32 [2, 3072], P(None, ('fsdp', 'tensor')), may hold values from 0.05 to 0.5
- gain_average: float32 [2, 3072], P(None, ('fsdp', 'tensor')), may hold values from 0.5 to 1.5
Outputs:
- train_weights: bfloat16 [2, 16896, 1536], P(None, 'tensor', 'fsdp')
- master_next: float32 [2, 16896, 1536], P(None, ('fsdp', 'tensor'))
- first_next: float32 [2, 16896, 1536], P(None, ('fsdp', 'tensor'))
- second_next: float32 [2, 16896, 1536], P(None, ('fsdp', 'tensor'))
- average_next: float32 [2, 16896, 1536], P(None, ('tensor', 'fsdp'))
- gain_weights: bfloat16 [2, 3072], replicated
- master_gains: float32 [2, 3072], P(None, ('fsdp', 'tensor'))
- first_gains: float32 [2, 3072], P(None, ('fsdp', 'tensor'))
- second_gains: float32 [2, 3072], P(None, ('fsdp', 'tensor'))
- average_gains: float32 [2, 3072], P(None, ('fsdp', 'tensor'))
All inputs are finite; a program needn't handle non-finite values.
Results may differ from a plain program's by a relative error of at most 0.001.
Values may be sent and summed in bfloat16 or wider, within the bound.
A program may use at most 128 MiB of HBM per device.

v0:
```python
import jax
import jax.numpy as jnp
from jax import lax
from jax.sharding import PartitionSpec as P

STEP = 20


learn_rate = 0.1
weight_decay = 0.1
beta_first = 0.9
beta_second = 0.95
adam_epsilon = 1e-08
average_decay = 0.9
clip_level = 0.5
mean_epsilon = 1e-06


def adam_step(gradient, master, first_state, second_state, clip_scale):
    clipped = gradient.astype(jnp.float32) * clip_scale
    first_new = beta_first * first_state + (1.0 - beta_first) * clipped
    second_new = beta_second * second_state + (1.0 - beta_second) * clipped * clipped
    first_fix = 1.0 - beta_first**STEP
    second_fix = 1.0 - beta_second**STEP
    direction = (
        first_new / first_fix / (jnp.sqrt(second_new / second_fix) + adam_epsilon)
        + weight_decay * master
    )
    master_new = master - learn_rate * direction
    return (master_new, first_new, second_new)


def on_device(
    grad_blocks,
    master_shard,
    first_moment,
    second_moment,
    average_shard,
    gain_grads,
    gain_master,
    gain_first,
    gain_second,
    gain_average,
):
    fsdp_count = lax.axis_size("fsdp")
    tensor_count = lax.axis_size("tensor")
    group_ratio = fsdp_count // tensor_count
    layer_count, block_rows, block_cols = grad_blocks.shape
    shard_rows = block_rows // fsdp_count
    width_full = block_cols * fsdp_count
    entries = (grad_blocks.size + gain_grads.size) * fsdp_count * tensor_count
    gain_wide = gain_grads.astype(jnp.float32)
    gain_squares = jnp.sum(gain_wide * gain_wide)
    sectioned = grad_blocks.reshape(layer_count, group_ratio, tensor_count, shard_rows, block_cols)
    arrived = lax.all_to_all(
        lax.all_to_all(sectioned, "tensor", split_axis=2, concat_axis=1, tiled=True),
        "fsdp",
        split_axis=1,
        concat_axis=4,
        tiled=True,
    )
    flat_grads = arrived.reshape(layer_count, shard_rows, width_full)
    flat_wide = flat_grads.astype(jnp.float32)
    total_squares = lax.psum(jnp.sum(flat_wide * flat_wide) + gain_squares, ("fsdp", "tensor"))
    clip_scale = jnp.minimum(1.0, clip_level / jnp.sqrt(total_squares / entries + mean_epsilon))
    master_next, first_next, second_next = adam_step(
        flat_grads, master_shard, first_moment, second_moment, clip_scale
    )
    master_gains, first_gains, second_gains = adam_step(
        gain_grads, gain_master, gain_first, gain_second, clip_scale
    )
    average_gains = average_decay * gain_average + (1.0 - average_decay) * master_gains
    outgoing = master_next.reshape(layer_count, 1, 1, shard_rows, width_full)
    home_float = lax.all_to_all(
        lax.all_to_all(
            outgoing.astype(jnp.bfloat16), "fsdp", split_axis=4, concat_axis=1, tiled=True
        ),
        "tensor",
        split_axis=1,
        concat_axis=2,
        tiled=True,
    ).astype(outgoing.dtype)
    train_float = home_float.reshape(layer_count, block_rows, block_cols)
    train_weights = train_float.astype(jnp.bfloat16)
    sorted_rows = train_float.reshape(layer_count, fsdp_count, shard_rows, block_cols)
    average_rows = lax.all_to_all(
        sorted_rows.astype(jnp.bfloat16), "fsdp", split_axis=1, concat_axis=3, tiled=True
    ).astype(sorted_rows.dtype)
    average_layout = average_rows.reshape(layer_count, shard_rows, width_full)
    average_next = average_decay * average_shard + (1.0 - average_decay) * average_layout
    gain_weights = lax.all_gather(
        master_gains.astype(jnp.bfloat16), ("fsdp", "tensor"), axis=1, tiled=True
    )
    return (
        train_weights,
        master_next,
        first_next,
        second_next,
        average_next,
        gain_weights,
        master_gains,
        first_gains,
        second_gains,
        average_gains,
    )


def solution(mesh):
    placed = (
        P(None, "tensor", "fsdp"),
        P(None, ("fsdp", "tensor"), None),
        P(None, ("fsdp", "tensor"), None),
        P(None, ("fsdp", "tensor"), None),
        P(None, ("tensor", "fsdp"), None),
        P(None, ("fsdp", "tensor")),
        P(None, ("fsdp", "tensor")),
        P(None, ("fsdp", "tensor")),
        P(None, ("fsdp", "tensor")),
        P(None, ("fsdp", "tensor")),
    )
    return jax.shard_map(
        on_device,
        mesh=mesh,
        in_specs=placed,
        out_specs=(
            P(None, "tensor", "fsdp"),
            P(None, ("fsdp", "tensor"), None),
            P(None, ("fsdp", "tensor"), None),
            P(None, ("fsdp", "tensor"), None),
            P(None, ("tensor", "fsdp"), None),
            P(),
            P(None, ("fsdp", "tensor")),
            P(None, ("fsdp", "tensor")),
            P(None, ("fsdp", "tensor")),
            P(None, ("fsdp", "tensor")),
        ),
        check_vma=False,
    )
```

profile of v0, /device:TPU:6, one launch (start us, length us, event | category | flops | bytes accessed | tf_op | source)
XLA Modules:
  0.0 250.7 jit_solution(17145453859018370600)
XLA Ops:
  0.6 5.4 %reshape.52 = bf16[2,2,8,132,96]{3,2,1,4,0:T(8,128)(2,1)S(1)} reshape(bf16[2,2112,96]{1,2,0:T(8,128)(2,1)} %param.10) | data formatting | bytes 1622016 | tf_op jit(solution)/shard_map/reshape | solution.py:54
  6.0 2.1 copy.92
  8.1 19.0 %all_to_all.75 = bf16[2,2,8,132,96]{4,1,3,0,2:T(2,128)(2,1)S(1)} all-to-all(bf16[2,2,8,132,96]{4,1,3,0,2:T(2,128)(2,1)S(1)} %copy.92), channel_id=1, replica_groups=mesh['fsdp'=16,'tensor'=8] {'tensor'}, dimensions={2} | all-to-all | bytes 1622016 | tf_op jit(solution)/shard_map/all_to_all | solution.py:56
  27.1 0.7 copy.93
  27.8 0.0 copy-start.6
  27.8 2.1 copy.94
  29.9 8.0 %all-to-all-start.1 = ((bf16[2,16,1,132,96]{4,0,3,2,1:T(2,128)(2,1)}), bf16[2,16,1,132,96]{4,0,3,2,1:T(2,128)(2,1)S(1)}, u32[]{:S(2)}, u32[]{:S(2)}) async-start(bf16[2,16,1,132,96]{4,0,3,2,1:T(2,128)(2,1)} %copy.94), calls=%async_computation.1 | async-start | bytes 2162688 | tf_op jit(solution)/shard_map/all_to_all | solution.py:55
  38.0 0.0 copy-done.6
  38.0 0.6 fusion.7
  38.6 17.5 %all-to-all-done.1 = bf16[2,16,1,132,96]{4,0,3,2,1:T(2,128)(2,1)S(1)} async-done(((bf16[2,16,1,132,96]{4,0,3,2,1:T(2,128)(2,1)}), bf16[2,16,1,132,96]{4,0,3,2,1:T(2,128)(2,1)S(1)}, u32[]{:S(2)}, u32[]{:S(2)}) %all-to-all-start.1) | async-done | bytes 811040 | tf_op jit(solution)/shard_map/all_to_all | solution.py:55
  56.1 2.8 %fusion = f32[]{:T(128)} fusion(bf16[2,16,1,132,96]{4,0,3,2,1:T(2,128)(2,1)S(1)} %all-to-all-done.1), kind=kLoop, calls=%fused_computation.3 | loop fusion | flops 1216511 | bytes 811012 | tf_op jit(solution)/shard_map/reduce_sum | solution.py:64
  60.3 62.3 %psum.7 = f32[]{:T(128)} all-reduce(f32[]{:T(128)S(6)} %add.44), channel_id=1, replica_groups=mesh['fsdp'=16,'tensor'=8] {'fsdp','tensor'}, use_global_device_ids=true, to_apply=%region_2.0 | all-reduce | flops 1 | bytes 8 | tf_op jit(solution)/shard_map/psum | solution.py:64
  123.2 0.7 fusion.1
  124.0 0.4 copy.95
  124.4 2.3 mul.112
  126.7 6.5 %convert_bitcast_fusion = (bf16[2,1,1,132,1536]{4,3,0,2,1:T(8,128)(2,1)}, f32[2,132,1536]{2,1,0:T(8,128)}, f32[2,132,1536]{2,1,0:T(8,128)}, f32[2,132,1536]{2,1,0:T(8,128)S(1)}) fusion(f32[2,132,1536]{2,0,1:T(2,128)} %param.11, f32[2,132,1536]{2,1,0:T(8,128)} %mul.112, f32[2,132,1536]{2,0,1:T(2,128)} %param.12, f32[2,132,1536]{2,0,1:T(2,128)} %param.13), kind=kLoop, calls=%fused_computation.14 | loop fusion | flops 6488064 | bytes 12165120 | tf_op jit(solution)/shard_map/convert_element_type | solution.py:76
  133.2 3.5 %copy.99 = bf16[2,1,1,132,1536]{3,0,2,1,4:T(2,128)(2,1)S(1)} copy(bf16[2,1,1,132,1536]{4,3,0,2,1:T(8,128)(2,1)} %get-tuple-element.74) | data formatting | bytes 1622016 | tf_op jit(solution)/shard_map/convert_element_type | solution.py:76
  136.8 26.7 %all_to_all.76 = bf16[2,1,1,132,1536]{3,0,2,1,4:T(2,128)(2,1)} all-to-all(bf16[2,1,1,132,1536]{3,0,2,1,4:T(2,128)(2,1)S(1)} %copy.99), channel_id=1, replica_groups=mesh['fsdp'=16,'tensor'=8] {'fsdp'}, dimensions={4} | all-to-all | bytes 1622016 | tf_op jit(solution)/shard_map/all_to_all | solution.py:75
  163.5 3.5 %copy.116 = bf16[2,1,1,132,16,96]{5,4,3,0,2,1:T(8,128)(2,1)S(1)} copy(bf16[2,1,1,132,16,96]{3,0,5,4,2,1:T(2,128)(2,1)} %bitcast.47) | data formatting | bytes 1622016 | tf_op jit(solution)/shard_map/all_to_all | solution.py:75
  167.0 1.1 copy.101
  168.1 19.0 %all_to_all.77 = bf16[2,16,1,132,96]{4,0,3,2,1:T(2,128)(2,1)S(1)} all-to-all(bf16[2,16,1,132,96]{4,0,3,2,1:T(2,128)(2,1)S(1)} %copy.101), channel_id=1, replica_groups=mesh['fsdp'=16,'tensor'=8] {'tensor'}, dimensions={1} | all-to-all | bytes 1622016 | tf_op jit(solution)/shard_map/all_to_all | solution.py:74
  187.2 0.1 copy.102
  187.3 0.1 copy.133
  187.5 2.1 copy.106
  189.5 4.6 %all-to-all-start.4 = ((bf16[2,16,132,96]{3,0,2,1:T(2,128)(2,1)}), bf16[2,16,132,96]{3,0,2,1:T(2,128)(2,1)}, u32[]{:S(2)}, u32[]{:S(2)}) async-start(bf16[2,16,132,96]{3,0,2,1:T(2,128)(2,1)} %copy.106), calls=%async_computation.4 | async-start | bytes 2162688 | tf_op jit(solution)/shard_map/all_to_all | solution.py:86
  194.2 0.0 copy-start
  194.2 4.0 %copy.110 = f32[2,132,1536]{2,0,1:T(2,128)} copy(f32[2,132,1536]{2,1,0:T(8,128)} %get-tuple-element.75) | data formatting | bytes 3244032
  198.2 0.0 copy-done
  198.2 2.4 copy.111
  200.6 0.0 copy-start.1
  200.6 0.0 copy-start.2
  200.6 2.4 copy.112
  203.0 0.0 copy-done.1
  203.0 0.0 copy-done.2
  203.0 0.0 copy-done.3
  203.0 0.0 copy-done.4
  203.0 0.6 multiply_add_fusion
  203.6 30.6 %all-gather = bf16[128,24,2]{1,2,0:T(2,128)(2,1)S(1)} all-gather(bf16[1,24,2]{1,2,0:T(2,128)(2,1)S(1)} %convert_bitcast_fusion.1), channel_id=1, replica_groups=mesh['fsdp'=16,'tensor'=8] {'fsdp','tensor'}, dimensions={0}, use_global_device_ids=true | all-gather | bytes 12384 | tf_op jit(solution)/shard_map/all_gather | solution.py:91
  234.2 0.7 reshape.51
  234.9 3.0 %copy.117 = bf16[2,2,8,1,132,96]{4,2,1,5,0,3:T(8,128)(2,1)S(1)} copy(bf16[2,2,8,1,132,96]{5,1,2,4,0,3:T(2,128)(2,1)S(1)} %bitcast.46) | data formatting | bytes 1622016
  237.9 2.9 %reshape.53 = bf16[2,2112,96]{1,2,0:T(8,128)(2,1)} reshape(bf16[2,2,8,1,132,96]{4,2,1,5,0,3:T(8,128)(2,1)S(1)} %copy.117) | data formatting | bytes 1622016
  240.8 0.0 copy-done.5
  240.8 0.0 all-to-all-done.4
  240.8 2.4 multiply_bitcast_fusion
  243.2 0.4 copy.107
  243.6 2.3 mul.125
  245.9 2.4 fusion.3
  248.2 2.4 copy.113
  (5 shorter events, 0.0 us)
Async XLA Ops:
  27.8 10.2 %copy-start.6 = (bf16[2,24]{1,0:T(2,128)(2,1)S(1)}, bf16[2,24]{1,0:T(2,128)(2,1)}, u32[]{:S(2)}) copy-start(bf16[2,24]{1,0:T(2,128)(2,1)} %param.15) | copy-start | bytes 292
  29.9 26.2 %all-to-all-start.1 = ((bf16[2,16,1,132,96]{4,0,3,2,1:T(2,128)(2,1)}), bf16[2,16,1,132,96]{4,0,3,2,1:T(2,128)(2,1)S(1)}, u32[]{:S(2)}, u32[]{:S(2)}) async-start(bf16[2,16,1,132,96]{4,0,3,2,1:T(2,128)(2,1)} %copy.94), calls=%async_computation.1 | async-start | bytes 2162688 | tf_op jit(solution)/shard_map/all_to_all | solution.py:55
  189.5 51.3 %all-to-all-start.4 = ((bf16[2,16,132,96]{3,0,2,1:T(2,128)(2,1)}), bf16[2,16,132,96]{3,0,2,1:T(2,128)(2,1)}, u32[]{:S(2)}, u32[]{:S(2)}) async-start(bf16[2,16,132,96]{3,0,2,1:T(2,128)(2,1)} %copy.106), calls=%async_computation.4 | async-start | bytes 2162688 | tf_op jit(solution)/shard_map/all_to_all | solution.py:86
  194.2 4.0 %copy-start = (f32[2,132,1536]{2,1,0:T(8,128)S(1)}, f32[2,132,1536]{2,1,0:T(8,128)}, u32[]{:S(2)}) copy-start(f32[2,132,1536]{2,1,0:T(8,128)} %get-tuple-element.76) | copy-start | bytes 4866052
  200.6 2.4 copy-start.1
  200.6 2.4 copy-start.2
  200.6 2.4 copy-start.3
  200.6 2.4 copy-start.4
  203.6 37.2 %copy-start.5 = (f32[2,24]{1,0:T(2,128)}, f32[2,24]{1,0:T(2,128)S(1)}, u32[]{:S(2)}) copy-start(f32[2,24]{1,0:T(2,128)S(1)} %get-tuple-element.71) | copy-start | bytes 580
where the time goes:
time: 255 us; the launch traced here: 251 us
  blocking collectives  158 us (62%)
  local copies, waits for them, and re-layouts  44 us (17%)
  waiting for transfers between devices  17.5 us (7%)
  other arithmetic  16 us (6%)
  starting transfers between devices  12.7 us (5%)
  between operations  2.8 us (1%)
    psum x1, blocking collectives, on_device(): lax.psum(jnp.sum(flat_wide * flat_wide) + gain_squares, ('fsdp', 'tensor'))  62.3 us
    all_gather x1, blocking collectives, on_device(): lax.all_gather(master_gains.astype(jnp.bfloat16), ('fsdp', 'tensor'), axi...  30.6 us
    all_to_all x1, blocking collectives, on_device(): lax.all_to_all(outgoing.astype(jnp.bfloat16), 'fsdp', split_axis=4, conca...  26.7 us
    all_to_all x1, blocking collectives, on_device(): lax.all_to_all(lax.all_to_all(outgoing.astype(jnp.bfloat16), 'fsdp', spli...  19 us
    all_to_all x1, blocking collectives, on_device(): lax.all_to_all(sectioned, 'tensor', split_axis=2, concat_axis=1, tiled=True)  19 us
    unnamed x21, local copies, waits for them, and re-layouts  17.9 us
    all_to_all x1, waiting for transfers between devices, on_device(): lax.all_to_all(lax.all_to_all(sectioned, 'tensor', split_axis=2, concat_a...  17.5 us
    all_to_all x1, starting transfers between devices, on_device(): lax.all_to_all(lax.all_to_all(sectioned, 'tensor', split_axis=2, concat_a...  8.05 us
  transfers between devices with their start and end apart: 2, of which 1 were waited for; matrix products, arithmetic and copies ran while one was open for 7% of the time, Pallas kernels for 0%

commit v1 on v0

v1 whole, which is shorter than its diff:
```python
import jax
import jax.numpy as jnp
from jax import lax
from jax.experimental import pallas as pl
from jax.experimental.pallas import tpu as pltpu
from jax.sharding import PartitionSpec as P

STEP = 20


learn_rate = 0.1
weight_decay = 0.1
beta_first = 0.9
beta_second = 0.95
adam_epsilon = 1e-08
average_decay = 0.9
clip_level = 0.5
mean_epsilon = 1e-06

MESH = pl.DeviceIdType.MESH
FSDP = 16
TENSOR = 8


def adam_step(gradient, master, first_state, second_state, clip_scale):
    clipped = gradient.astype(jnp.float32) * clip_scale
    first_new = beta_first * first_state + (1.0 - beta_first) * clipped
    second_new = beta_second * second_state + (1.0 - beta_second) * clipped * clipped
    first_fix = 1.0 - beta_first**STEP
    second_fix = 1.0 - beta_second**STEP
    direction = (
        first_new / first_fix / (jnp.sqrt(second_new / second_fix) + adam_epsilon)
        + weight_decay * master
    )
    master_new = master - learn_rate * direction
    return (master_new, first_new, second_new)


def enter(f, t):
    barrier = pltpu.get_barrier_semaphore()

    @pl.loop(1, TENSOR)
    def _(i):
        pl.semaphore_signal(
            barrier, inc=1, device_id=(f, lax.rem(t + i, TENSOR)), device_id_type=MESH
        )

    @pl.loop(1, FSDP)
    def _(i):
        pl.semaphore_signal(
            barrier, inc=1, device_id=(lax.rem(f + i, FSDP), t), device_id_type=MESH
        )

    pl.semaphore_wait(barrier, TENSOR + FSDP - 2)


def remote(source, target, send_sem, recv_sem, device):
    return pltpu.make_async_remote_copy(
        src_ref=source,
        dst_ref=target,
        send_sem=send_sem,
        recv_sem=recv_sem,
        device_id=device,
        device_id_type=MESH,
    )


def send(source, target, send_sem, recv_sem, device, is_own):
    @pl.when(is_own)
    def _():
        pltpu.make_async_copy(source, target, recv_sem).start()

    @pl.when(jnp.logical_not(is_own))
    def _():
        remote(source, target, send_sem, recv_sem, device).start()


def sent(source, target, send_sem, recv_sem, device, is_own):
    @pl.when(jnp.logical_not(is_own))
    def _():
        remote(source, target, send_sem, recv_sem, device).wait_send()


def arrived(target, recv_sem):
    pltpu.make_async_copy(target, target, recv_sem).wait()


def small_copies(f, t, small_ref, all_ref, sems):
    row_send, row_recv, col_send, col_recv = sems

    def row_copy(i):
        return remote(
            small_ref,
            all_ref.at[f, t],
            row_send.at[i],
            row_recv.at[t],
            (f, lax.rem(t + i, TENSOR)),
        )

    def col_copy(i):
        return remote(
            all_ref.at[f],
            all_ref.at[f],
            col_send.at[i],
            col_recv.at[f],
            (lax.rem(f + i, FSDP), t),
        )

    return row_copy, col_copy


def small_first(f, t, small_ref, all_ref, sems):
    row_copy, _ = small_copies(f, t, small_ref, all_ref, sems)
    pltpu.make_async_copy(small_ref, all_ref.at[f, t], sems[1].at[t]).start()

    @pl.loop(1, TENSOR)
    def _(i):
        row_copy(i).start()


def small_second(f, t, small_ref, all_ref, sems):
    _, col_copy = small_copies(f, t, small_ref, all_ref, sems)

    @pl.loop(0, TENSOR)
    def _(i):
        arrived(all_ref.at[f, i], sems[1].at[i])

    @pl.loop(1, FSDP)
    def _(i):
        col_copy(i).start()


def small_done(f, t, small_ref, all_ref, sems):
    row_copy, col_copy = small_copies(f, t, small_ref, all_ref, sems)

    @pl.loop(1, FSDP)
    def _(i):
        source = lax.rem(f + i, FSDP)
        arrived(all_ref.at[source], sems[3].at[source])

    @pl.loop(1, TENSOR)
    def _(i):
        row_copy(i).wait_send()

    @pl.loop(1, FSDP)
    def _(i):
        col_copy(i).wait_send()


def gather_kernel(
    wire, small, out, sums, mid, send_a, recv_a, send_b, recv_b, rs, rr, cs, cr
):
    f = lax.axis_index("fsdp")
    t = lax.axis_index("tensor")
    sems = (rs, rr, cs, cr)
    enter(f, t)
    small_first(f, t, small, sums, sems)
    small_second(f, t, small, sums, sems)

    def stage_a(n):
        i, half = n // 2, lax.rem(n + f // TENSOR, 2)
        to = lax.rem(t + i + f, TENSOR)
        k = half * TENSOR + to
        slot = 2 * t + half
        return (
            wire.at[k], mid.at[slot], send_a.at[k], recv_a.at[slot], (f, to), to == t,
        )

    def stage_b(n):
        i, half = n // 2, lax.rem(n + f // TENSOR, 2)
        m = 2 * lax.rem(t - i - f + 4 * TENSOR, TENSOR) + half
        return m, (mid.at[m], out.at[f], send_b.at[m], recv_b.at[f], (m, t), m == f)

    @pl.loop(0, FSDP)
    def _(n):
        send(*stage_a(n))

    @pl.loop(0, FSDP)
    def _(n):
        m, copy = stage_b(n)
        arrived(mid.at[m], recv_a.at[m])
        send(*copy)

    @pl.loop(0, FSDP)
    def _(n):
        arrived(out.at[n], recv_b.at[n])

    small_done(f, t, small, sums, sems)

    @pl.loop(0, FSDP)
    def _(n):
        sent(*stage_a(n))
        sent(*stage_b(n)[1])


def spread_kernel(
    wire, small, train, average, gains, mid,
    send_a, recv_a, send_b, recv_b, send_c, recv_c, rs, rr, cs, cr,
):
    f = lax.axis_index("fsdp")
    t = lax.axis_index("tensor")
    sems = (rs, rr, cs, cr)
    enter(f, t)
    small_first(f, t, small, gains, sems)

    def stage_a(n):
        j = lax.rem(f + n + 2 * t, FSDP)
        return (wire.at[j], mid.at[f], send_a.at[j], recv_a.at[f], (j, t), j == f)

    def stage_b(n):
        source = lax.rem(f - n - 2 * t + 2 * FSDP, FSDP)
        to = source // 2
        k = lax.rem(source, 2) * TENSOR + t
        return source, (
            mid.at[source], train.at[k], send_b.at[source], recv_b.at[k], (f, to), to == t,
        )

    def stage_c(n):
        k = lax.rem(n, 2) * TENSOR + lax.rem(n // 2 + f + t, TENSOR)
        return k, (train.at[k], average.at[f], send_c.at[k], recv_c.at[f], (k, t), k == f)

    @pl.loop(0, FSDP)
    def _(n):
        send(*stage_a(n))

    @pl.loop(0, FSDP)
    def _(n):
        source, copy = stage_b(n)
        arrived(mid.at[source], recv_a.at[source])
        send(*copy)

    small_second(f, t, small, gains, sems)

    @pl.loop(0, FSDP)
    def _(n):
        k, copy = stage_c(n)
        arrived(train.at[k], recv_b.at[k])
        send(*copy)

    @pl.loop(0, FSDP)
    def _(n):
        arrived(average.at[n], recv_c.at[n])

    small_done(f, t, small, gains, sems)

    @pl.loop(0, FSDP)
    def _(n):
        sent(*stage_a(n))
        sent(*stage_b(n)[1])
        sent(*stage_c(n)[1])


def exchange(kernel, wire, small, outputs, stages, collective_id):
    vmem = pl.BlockSpec(memory_space=pltpu.VMEM)
    pieces = jax.ShapeDtypeStruct(wire.shape, wire.dtype)
    dma = pltpu.SemaphoreType.DMA
    return pl.pallas_call(
        kernel,
        out_shape=[pieces] * outputs
        + [jax.ShapeDtypeStruct((FSDP, TENSOR) + small.shape, small.dtype)],
        in_specs=[vmem] * 2,
        out_specs=[vmem] * (outputs + 1),
        scratch_shapes=[pltpu.VMEM(wire.shape, wire.dtype)]
        + [dma((FSDP,))] * (2 * stages)
        + [dma((TENSOR,)), dma((TENSOR,)), dma((FSDP,)), dma((FSDP,))],
        compiler_params=pltpu.CompilerParams(
            collective_id=collective_id, has_side_effects=True
        ),
    )(wire, small)


def on_device(
    grad_blocks,
    master_shard,
    first_moment,
    second_moment,
    average_shard,
    gain_grads,
    gain_master,
    gain_first,
    gain_second,
    gain_average,
):
    layers, block_rows, block_cols = grad_blocks.shape
    rows = block_rows // FSDP
    width = block_cols * FSDP
    entries = (grad_blocks.size + gain_grads.size) * FSDP * TENSOR

    wide = grad_blocks.astype(jnp.float32)
    gain_wide = gain_grads.astype(jnp.float32)
    squares = jnp.sum(wide * wide) + jnp.sum(gain_wide * gain_wide)
    small = jnp.pad(squares.reshape(1, 1), ((0, 0), (0, 127)))
    wire = grad_blocks.reshape(layers, FSDP, rows, block_cols).transpose(1, 0, 2, 3)
    pieces, sums = exchange(gather_kernel, wire, small, 1, 2, 0)
    total_squares = jnp.sum(sums)
    clip_scale = jnp.minimum(1.0, clip_level / jnp.sqrt(total_squares / entries + mean_epsilon))

    def turned(x):
        return x.transpose(1, 0, 2)

    grads = pieces.transpose(2, 1, 0, 3).reshape(rows, layers, width)
    master_next, first_next, second_next = adam_step(
        grads, turned(master_shard), turned(first_moment), turned(second_moment), clip_scale
    )
    master_gains, first_gains, second_gains = adam_step(
        gain_grads, gain_master, gain_first, gain_second, clip_scale
    )
    average_gains = average_decay * gain_average + (1.0 - average_decay) * master_gains

    gain_count = gain_grads.size
    gain_cols = gain_grads.shape[1]
    gain_small = jnp.pad(
        master_gains.astype(jnp.bfloat16).astype(jnp.float32).reshape(1, gain_count),
        ((0, 0), (0, 128 - gain_count)),
    )
    out_wire = (
        master_next.astype(jnp.bfloat16)
        .reshape(rows, layers, FSDP, block_cols)
        .transpose(2, 1, 0, 3)
    )
    train, averages, gains = exchange(spread_kernel, out_wire, gain_small, 2, 3, 1)
    train_weights = train.transpose(1, 0, 2, 3).reshape(layers, block_rows, block_cols)
    layout = averages.transpose(2, 1, 0, 3).reshape(rows, layers, width).astype(jnp.float32)
    average_next = average_decay * turned(average_shard) + (1.0 - average_decay) * layout
    gain_weights = (
        gains.reshape(FSDP * TENSOR, 128)[:, :gain_count]
        .reshape(FSDP * TENSOR, layers, gain_cols)
        .transpose(1, 0, 2)
        .reshape(layers, FSDP * TENSOR * gain_cols)
        .astype(jnp.bfloat16)
    )
    return (
        train_weights,
        turned(master_next),
        turned(first_next),
        turned(second_next),
        turned(average_next),
        gain_weights,
        master_gains,
        first_gains,
        second_gains,
        average_gains,
    )


def solution(mesh):
    flat = P(None, ("fsdp", "tensor"), None)
    gain = P(None, ("fsdp", "tensor"))
    blocks = P(None, "tensor", "fsdp")
    averaging = P(None, ("tensor", "fsdp"), None)
    return jax.shard_map(
        on_device,
        mesh=mesh,
        in_specs=(blocks, flat, flat, flat, averaging, gain, gain, gain, gain, gain),
        out_specs=(blocks, flat, flat, flat, averaging, P(), gain, gain, gain, gain),
        check_vma=False,
    )
```

time: 255 us -> 144 us (0.56); the launches traced: 251 us -> 144 us
  blocking collectives: 158 us -> 0 us
  Pallas kernels: 0 us -> 86.3 us
  waiting for transfers between devices: 17.5 us -> 0 us
  starting transfers between devices: 12.7 us -> 0 us
  local copies, waits for them, and re-layouts: 44 us -> 38.2 us
    pallas_call x0 -> x2, Pallas kernels: none -> 86.3 us  [exchange(): pl.pallas_call(kernel, out_shape=[pieces] * outputs + [jax.ShapeDtypeStru...]
    all_to_all x3 -> x0, blocking collectives: 64.7 us -> none  [the longest x1 26.7 us: on_device(): lax.all_to_all(outgoing.astype(jnp.bfloat16), 'fsdp', split_axis=4, conca...]
    psum x1 -> x0, blocking collectives: 62.3 us -> none  [on_device(): lax.psum(jnp.sum(flat_wide * flat_wide) + gain_squares, ('fsdp', 'tensor'))]
    all_gather x1 -> x0, blocking collectives: 30.6 us -> none  [on_device(): lax.all_gather(master_gains.astype(jnp.bfloat16), ('fsdp', 'tensor'), axi...]
    all_to_all x2 -> x0, waiting for transfers between devices: 17.5 us -> none  [the longest x1 17.5 us: on_device(): lax.all_to_all(lax.all_to_all(sectioned, 'tensor', split_axis=2, concat_a...]
    all_to_all x2 -> x0, starting transfers between devices: 12.7 us -> none  [the longest x1 8.05 us: on_device(): lax.all_to_all(lax.all_to_all(sectioned, 'tensor', split_axis=2, concat_a...]
    all_to_all x7 -> x0, local copies, waits for them, and re-layouts: 9.83 us -> none  [the longest x2 4.62 us: on_device(): lax.all_to_all(outgoing.astype(jnp.bfloat16), 'fsdp', split_axis=4, conca...]
    reshape x2 -> x5, local copies, waits for them, and re-layouts: 7.46 us -> 13.2 us  [the longest x2 7.59 us: on_device(): grad_blocks.reshape(layers, FSDP, rows, block_cols).transpose(1, 0, 2, 3)]
  transfers between devices with their start and end apart: 2 -> 0, of which waited for: 1 -> 0; matrix products, arithmetic and copies ran while one was open for 7% -> 0% of each run, Pallas kernels for 0% -> 0%
where the time goes in v1:
time: 144 us
  Pallas kernels  86.3 us (60%)
  local copies, waits for them, and re-layouts  38.2 us (27%)
  other arithmetic  16.4 us (11%)
  between operations  2.8 us (2%)
    pallas_call x2, Pallas kernels, exchange(): pl.pallas_call(kernel, out_shape=[pieces] * outputs + [jax.ShapeDtypeStru...  86.3 us
    unnamed x21, local copies, waits for them, and re-layouts  17.6 us
    reshape x2, local copies, waits for them, and re-layouts, on_device(): grad_blocks.reshape(layers, FSDP, rows, block_cols).transpose(1, 0, 2, 3)  7.59 us
    reshape x2, local copies, waits for them, and re-layouts, on_device(): out_wire = master_next.astype(jnp.bfloat16).reshape(rows, layers, FSDP, b...  5.5 us
    convert_element_type x1, other arithmetic, on_device(): master_next.astype(jnp.bfloat16).reshape(rows, layers, FSDP, block_cols)  5.46 us
    reduce_sum x2, other arithmetic, on_device(): squares = jnp.sum(wide * wide) + jnp.sum(gain_wide * gain_wide)  3.45 us
    mul x2, local copies, waits for them, and re-layouts, adam_step(): clipped = gradient.astype(jnp.float32) * clip_scale  2.98 us
    mul x2, local copies, waits for them, and re-layouts, on_device(): (1.0 - average_decay) * layout  2.98 us

profile of v1, /device:TPU:6, one launch (start us, length us, event | category | flops | bytes accessed | tf_op | source)
XLA Modules:
  0.0 143.8 jit_solution(15830660549086684836)
XLA Ops:
  0.6 1.3 fusion.8
  1.9 2.2 %multiply_reduce_fusion = f32[]{:T(128)} fusion(bf16[2,2112,96]{1,2,0:T(8,128)(2,1)} %param.10), kind=kLoop, calls=%fused_computation.14 | loop fusion | flops 1216511 | bytes 811012 | tf_op jit(solution)/shard_map/reduce_sum | solution.py:291
  5.4 0.5 pad.10.small
  5.9 5.4 %reshape.58 = bf16[2,16,132,96]{2,1,3,0:T(8,128)(2,1)S(1)} reshape(bf16[2,2112,96]{1,2,0:T(8,128)(2,1)} %param.10) | data formatting | bytes 1622016 | tf_op jit(solution)/shard_map/reshape | solution.py:293
  11.3 0.0 copy-start.1
  11.3 0.0 copy-start.2
  11.3 0.0 copy-start.3
  11.3 0.0 copy-start.4
  11.4 0.0 copy-start.6
  11.4 2.2 %copy.24 = bf16[2,16,132,96]{3,2,0,1:T(8,128)(2,1)} copy(bf16[2,16,132,96]{2,1,3,0:T(8,128)(2,1)S(1)} %reshape.58) | data formatting | bytes 1622016 | tf_op jit(solution)/shard_map/reshape | solution.py:293
  13.6 39.5 %shard_map.177 = (bf16[16,2,132,96]{3,2,1,0:T(8,128)(2,1)}, f32[16,8,1,128]{3,2,1,0:T(1,128)}) custom-call(bf16[16,2,132,96]{3,2,1,0:T(8,128)(2,1)} %bitcast.70, f32[1,128]{1,0:T(1,128)} %pad.10.small), custom_call_target="tpu_custom_call" | custom-call | tf_op jit(solution)/shard_map/pallas_call | solution.py:257
  53.0 1.6 %reduce_sum.29 = f32[]{:T(128)} reduce(f32[16,8,1,128]{3,2,1,0:T(1,128)} %get-tuple-element.16, f32[]{:T(128)} %constant.14.clone.1), dimensions={0,1,2,3}, to_apply=%region_2.3 | reduce | flops 16383 | bytes 65544 | tf_op jit(solution)/shard_map/reduce_sum | solution.py:295
  55.3 0.0 copy-done.1
  55.3 0.0 copy-done.2
  55.3 0.0 copy-done.3
  55.3 0.0 copy-done.4
  55.4 0.0 copy-done.6
  55.4 0.6 multiply_add_fusion
  56.0 0.0 copy-start.5
  56.0 0.1 reshape.55
  56.1 0.5 pad_convert_fusion.small
  56.6 1.4 multiply_bitcast_fusion.1
  58.0 0.0 copy-done.5
  58.0 0.7 copy.25
  58.7 2.3 %mul.112 = f32[132,2,1536]{2,0,1:T(8,128)} reshape(f32[132,2,16,96]{3,2,0,1:T(8,128)S(1)} %copy.25) | data formatting | bytes 3244032 | tf_op jit(solution)/shard_map/mul | solution.py:26
  61.0 5.5 %fusion.12 = (bf16[132,2,1536]{2,0,1:T(8,128)(2,1)}, f32[132,2,1536]{2,0,1:T(8,128)S(1)}, f32[2,132,1536]{2,1,0:T(8,128)S(1)}, f32[2,132,1536]{2,1,0:T(8,128)S(1)}) fusion(f32[132,2,1536]{2,0,1:T(8,128)} %mul.112, f32[2,132,1536]{2,0,1:T(2,128)} %param.13, f32[2,132,1536]{2,0,1:T(2,128)} %param.12, f32[2,132,1536]{2,0,1:T(2,128)} %param.11), kind=kLoop, calls=%fused_computation.29 | loop fusion | flops 6488064 | bytes 12165120 | tf_op jit(solution)/shard_map/convert_element_type | solution.py:317
  66.4 2.4 %copy.34 = f32[2,132,1536]{2,0,1:T(2,128)} copy(f32[2,132,1536]{2,1,0:T(8,128)S(1)} %bitcast.68) | data formatting | bytes 3244032
  68.8 3.0 %reshape.54 = bf16[132,2,16,96]{3,2,0,1:T(8,128)(2,1)} reshape(bf16[132,2,1536]{2,0,1:T(8,128)(2,1)} %get-tuple-element.34) | data formatting | bytes 1622016 | tf_op jit(solution)/shard_map/reshape | solution.py:318
  71.8 2.5 %copy.66 = bf16[132,2,16,96]{3,0,1,2:T(8,128)(2,1)} copy(bf16[132,2,16,96]{3,2,0,1:T(8,128)(2,1)} %reshape.54) | data formatting | bytes 1622016 | tf_op jit(solution)/shard_map/reshape | solution.py:318
  74.3 46.8 %shard_map.178 = (bf16[16,2,132,96]{3,2,1,0:T(8,128)(2,1)}, bf16[16,2,132,96]{3,2,1,0:T(8,128)(2,1)}, f32[16,8,1,128]{3,2,1,0:T(1,128)}) custom-call(bf16[16,2,132,96]{3,2,1,0:T(8,128)(2,1)} %bitcast.69, f32[1,128]{1,0:T(1,128)} %pad_convert_fusion.small), custom_call_target="tpu_custom_call" | custom-call | tf_op jit(solution)/shard_map/pallas_call | solution.py:257
  121.2 0.9 convert.7
  122.1 0.1 copy.31
  122.2 0.1 copy.32
  122.3 0.7 convert_element_type.46
  123.1 4.0 %copy.40 = bf16[2,16,132,96]{2,1,3,0:T(8,128)(2,1)} copy(bf16[2,16,132,96]{3,2,0,1:T(8,128)(2,1)} %bitcast.71) | data formatting | bytes 1622016
  127.1 3.9 %reshape.59 = bf16[2,2112,96]{1,2,0:T(8,128)(2,1)} reshape(bf16[2,16,132,96]{2,1,3,0:T(8,128)(2,1)} %copy.40) | data formatting | bytes 1622016
  131.0 2.4 %copy.36 = f32[2,132,1536]{2,0,1:T(2,128)} copy(f32[2,132,1536]{2,1,0:T(8,128)S(1)} %get-tuple-element.36) | data formatting | bytes 3244032
  133.4 0.0 copy-start
  133.4 2.4 %copy.35 = f32[2,132,1536]{2,0,1:T(2,128)} copy(f32[2,132,1536]{2,1,0:T(8,128)S(1)} %get-tuple-element.37) | data formatting | bytes 3244032
  135.8 0.0 copy-done
  135.8 0.2 multiply_bitcast_fusion
  136.0 0.7 copy.30
  136.7 2.3 %mul.137 = f32[132,2,1536]{2,0,1:T(8,128)} reshape(f32[132,2,16,96]{3,2,0,1:T(8,128)S(1)} %copy.30) | data formatting | bytes 3244032 | tf_op jit(solution)/shard_map/mul | solution.py:324
  139.0 2.4 %fusion.1 = f32[2,132,1536]{2,1,0:T(8,128)S(1)} fusion(f32[132,2,1536]{2,0,1:T(8,128)} %mul.137, f32[2,132,1536]{2,0,1:T(2,128)} %param.14), kind=kLoop, calls=%fused_computation.5 | loop fusion | flops 811008 | bytes 4866048 | tf_op jit(solution)/shard_map/transpose | solution.py:299
  141.4 2.4 %copy.37 = f32[2,132,1536]{2,0,1:T(2,128)} copy(f32[2,132,1536]{2,1,0:T(8,128)S(1)} %fusion.1) | data formatting | bytes 3244032
  (2 shorter events, 0.0 us)
Async XLA Ops:
  11.3 44.0 %copy-start.1 = (f32[2,24]{1,0:T(2,128)S(1)}, f32[2,24]{1,0:T(2,128)}, u32[]{:S(2)}) copy-start(f32[2,24]{1,0:T(2,128)} %param.19) | copy-start | bytes 580
  11.3 44.0 %copy-start.2 = (f32[2,24]{1,0:T(2,128)S(1)}, f32[2,24]{1,0:T(2,128)}, u32[]{:S(2)}) copy-start(f32[2,24]{1,0:T(2,128)} %param.16) | copy-start | bytes 580
  11.3 44.0 %copy-start.3 = (f32[2,24]{1,0:T(2,128)S(1)}, f32[2,24]{1,0:T(2,128)}, u32[]{:S(2)}) copy-start(f32[2,24]{1,0:T(2,128)} %param.17) | copy-start | bytes 580
  11.3 44.0 %copy-start.4 = (f32[2,24]{1,0:T(2,128)S(1)}, f32[2,24]{1,0:T(2,128)}, u32[]{:S(2)}) copy-start(f32[2,24]{1,0:T(2,128)} %param.18) | copy-start | bytes 580
  11.4 44.0 %copy-start.6 = (bf16[2,24]{1,0:T(2,128)(2,1)S(1)}, bf16[2,24]{1,0:T(2,128)(2,1)}, u32[]{:S(2)}) copy-start(bf16[2,24]{1,0:T(2,128)(2,1)} %param.15) | copy-start | bytes 292
  56.0 2.0 %copy-start.5 = (f32[2,24]{1,0:T(2,128)}, f32[2,24]{1,0:T(2,128)S(1)}, u32[]{:S(2)}) copy-start(f32[2,24]{1,0:T(2,128)S(1)} %get-tuple-element.31) | copy-start | bytes 580
  133.4 2.4 %copy-start = (bf16[16,2,132,96]{3,2,1,0:T(8,128)(2,1)S(1)}, bf16[16,2,132,96]{3,2,1,0:T(8,128)(2,1)}, u32[]{:S(2)}) copy-start(bf16[16,2,132,96]{3,2,1,0:T(8,128)(2,1)} %get-tuple-element.18) | copy-start | bytes 2433028

commit v2 on v1

--- a/solution.py
+++ b/solution.py
@@ -20,6 +20,7 @@
 MESH = pl.DeviceIdType.MESH
 FSDP = 16
 TENSOR = 8
+SPAN = 384
 
 
 def adam_step(gradient, master, first_state, second_state, clip_scale):
@@ -269,6 +270,85 @@
     )(wire, small)
 
 
+def joined(pieces, group, layer):
+    return jnp.concatenate(
+        [pieces[4 * group + i, layer].astype(jnp.float32) for i in range(4)], axis=1
+    )
+
+
+def part(ref, buf, sem, layer, group, out):
+    span = pl.ds(group * SPAN, SPAN)
+    there, here = ref.at[:, layer, span], buf.at[layer, :, span]
+    if out:
+        there, here = here, there
+    return pltpu.make_async_copy(there, here, sem.at[layer, group])
+
+
+STEPS = [(layer, group) for layer in range(2) for group in range(4)]
+
+
+def update_kernel(
+    pieces, scale, master, first, second,
+    out_wire, master_out, first_out, second_out,
+    master_buf, first_buf, second_buf, *sems,
+):
+    cols = pieces.shape[3]
+    refs = (master, first, second)
+    outs = (master_out, first_out, second_out)
+    bufs = (master_buf, first_buf, second_buf)
+    clip_scale = scale[0, 0]
+    for step in STEPS:
+        for i in range(3):
+            part(refs[i], bufs[i], sems[i], *step, False).start()
+    for layer, group in STEPS:
+        span = slice(group * SPAN, (group + 1) * SPAN)
+        grads = joined(pieces, group, layer)
+        for i in range(3):
+            part(refs[i], bufs[i], sems[i], layer, group, False).wait()
+        news = adam_step(grads, *[buf[layer, :, span] for buf in bufs], clip_scale)
+        for i in range(3):
+            bufs[i][layer, :, span] = news[i]
+            part(outs[i], bufs[i], sems[3 + i], layer, group, True).start()
+        for i in range(4):
+            out_wire[4 * group + i, layer] = news[0][:, i * cols : (i + 1) * cols].astype(
+                out_wire.dtype
+            )
+    for step in STEPS:
+        for i in range(3):
+            part(outs[i], bufs[i], sems[3 + i], *step, True).wait()
+
+
+def average_kernel(pieces, average, average_out, buf, sem, sem_out):
+    for step in STEPS:
+        part(average, buf, sem, *step, False).start()
+    for layer, group in STEPS:
+        span = slice(group * SPAN, (group + 1) * SPAN)
+        news = joined(pieces, group, layer)
+        part(average, buf, sem, layer, group, False).wait()
+        buf[layer, :, span] = (
+            average_decay * buf[layer, :, span] + (1.0 - average_decay) * news
+        )
+        part(average_out, buf, sem_out, layer, group, True).start()
+    for step in STEPS:
+        part(average_out, buf, sem_out, *step, True).wait()
+
+
+def turned(x):
+    return x.transpose(1, 0, 2)
+
+
+def plain(kernel, outputs, out_specs, operands, specs, states):
+    shape = (2, outputs[-1].shape[0], 4 * SPAN)
+    return pl.pallas_call(
+        kernel,
+        out_shape=outputs,
+        in_specs=specs,
+        out_specs=out_specs,
+        scratch_shapes=[pltpu.VMEM(shape, jnp.float32)] * states
+        + [pltpu.SemaphoreType.DMA((2, 4))] * (2 * states),
+    )(*operands)
+
+
 def on_device(
     grad_blocks,
     master_shard,
@@ -295,12 +375,24 @@
     total_squares = jnp.sum(sums)
     clip_scale = jnp.minimum(1.0, clip_level / jnp.sqrt(total_squares / entries + mean_epsilon))
 
-    def turned(x):
-        return x.transpose(1, 0, 2)
-
-    grads = pieces.transpose(2, 1, 0, 3).reshape(rows, layers, width)
-    master_next, first_next, second_next = adam_step(
-        grads, turned(master_shard), turned(first_moment), turned(second_moment), clip_scale
+    vmem = pl.BlockSpec(memory_space=pltpu.VMEM)
+    smem = pl.BlockSpec(memory_space=pltpu.SMEM)
+    far = pl.BlockSpec(memory_space=pl.ANY)
+    flat = jax.ShapeDtypeStruct((rows, layers, width), jnp.float32)
+    wire_out = jax.ShapeDtypeStruct(wire.shape, wire.dtype)
+    out_wire, master_next, first_next, second_next = plain(
+        update_kernel,
+        [wire_out, flat, flat, flat],
+        [vmem, far, far, far],
+        (
+            pieces,
+            clip_scale.reshape(1, 1),
+            turned(master_shard),
+            turned(first_moment),
+            turned(second_moment),
+        ),
+        [vmem, smem, far, far, far],
+        3,
     )
     master_gains, first_gains, second_gains = adam_step(
         gain_grads, gain_master, gain_first, gain_second, clip_scale
@@ -313,15 +405,11 @@
         master_gains.astype(jnp.bfloat16).astype(jnp.float32).reshape(1, gain_count),
         ((0, 0), (0, 128 - gain_count)),
     )
-    out_wire = (
-        master_next.astype(jnp.bfloat16)
-        .reshape(rows, layers, FSDP, block_cols)
-        .transpose(2, 1, 0, 3)
-    )
     train, averages, gains = exchange(spread_kernel, out_wire, gain_small, 2, 3, 1)
     train_weights = train.transpose(1, 0, 2, 3).reshape(layers, block_rows, block_cols)
-    layout = averages.transpose(2, 1, 0, 3).reshape(rows, layers, width).astype(jnp.float32)
-    average_next = average_decay * turned(average_shard) + (1.0 - average_decay) * layout
+    (average_next,) = plain(
+        average_kernel, [flat], [far], (averages, turned(average_shard)), [vmem, far], 1
+    )
     gain_weights = (
         gains.reshape(FSDP * TENSOR, 128)[:, :gain_count]
         .reshape(FSDP * TENSOR, layers, gain_cols)

time: 144 us -> 124 us (0.86)
  local copies, waits for them, and re-layouts: 38.2 us -> 15.3 us
  Pallas kernels: 86.3 us -> 98 us
  other arithmetic: 16.4 us -> 7.03 us
    pallas_call x0 -> x2, Pallas kernels: none -> 11.7 us  [plain(): pl.pallas_call(kernel, out_shape=outputs, in_specs=specs, out_specs=out_s...]
    unnamed x21 -> x15, local copies, waits for them, and re-layouts: 17.6 us -> 6.19 us
    mul x4 -> x0, local copies, waits for them, and re-layouts: 5.96 us -> none  [the longest x2 2.98 us: adam_step(): clipped = gradient.astype(jnp.float32) * clip_scale]
    reshape x2 -> x0, local copies, waits for them, and re-layouts: 5.5 us -> none  [on_device(): out_wire = master_next.astype(jnp.bfloat16).reshape(rows, layers, FSDP, b...]
    convert_element_type x1 -> x0, other arithmetic: 5.46 us -> none  [on_device(): master_next.astype(jnp.bfloat16).reshape(rows, layers, FSDP, block_cols)]
    transpose x1 -> x0, other arithmetic: 2.37 us -> none  [turned(): return x.transpose(1, 0, 2)]
    mul x2 -> x0, other arithmetic: 1.56 us -> none  [the longest x1 1.39 us: adam_step(): clipped = gradient.astype(jnp.float32) * clip_scale]
where the time goes in v2:
time: 124 us; the launch traced here: 123 us
  Pallas kernels  98 us (79%)
  local copies, waits for them, and re-layouts  15.3 us (12%)
  other arithmetic  7.03 us (6%)
  between operations  2.79 us (2%)
    pallas_call x2, Pallas kernels, exchange(): pl.pallas_call(kernel, out_shape=[pieces] * outputs + [jax.ShapeDtypeStru...  86.3 us
    pallas_call x2, Pallas kernels, plain(): pl.pallas_call(kernel, out_shape=outputs, in_specs=specs, out_specs=out_s...  11.7 us
    reshape x2, local copies, waits for them, and re-layouts, on_device(): grad_blocks.reshape(layers, FSDP, rows, block_cols).transpose(1, 0, 2, 3)  7.59 us
    unnamed x15, local copies, waits for them, and re-layouts  6.19 us
    reduce_sum x2, other arithmetic, on_device(): squares = jnp.sum(wide * wide) + jnp.sum(gain_wide * gain_wide)  3.45 us

profile of v2, /device:TPU:6, one launch (start us, length us, event | category | flops | bytes accessed | tf_op | source)
XLA Modules:
  0.0 123.1 jit_solution(16407855140136555809)
XLA Ops:
  0.6 1.3 %fusion.2 = f32[]{:T(128)} fusion(bf16[2,24]{1,0:T(2,128)(2,1)} %param.15), kind=kLoop, calls=%fused_computation.7 | loop fusion | flops 143 | bytes 100 | tf_op jit(solution)/shard_map/reduce_sum | solution.py:371
  1.9 2.2 %multiply_reduce_fusion = f32[]{:T(128)} fusion(bf16[2,2112,96]{1,2,0:T(8,128)(2,1)} %param.10), kind=kLoop, calls=%fused_computation | loop fusion | flops 1216511 | bytes 811012 | tf_op jit(solution)/shard_map/reduce_sum | solution.py:371
  5.4 0.5 pad.10.small
  5.9 5.4 %reshape.50 = bf16[2,16,132,96]{2,1,3,0:T(8,128)(2,1)S(1)} reshape(bf16[2,2112,96]{1,2,0:T(8,128)(2,1)} %param.10) | data formatting | bytes 1622016 | tf_op jit(solution)/shard_map/reshape | solution.py:373
  11.3 0.0 copy-start
  11.3 0.0 copy-start.1
  11.3 0.0 copy-start.2
  11.3 0.0 copy-start.3
  11.4 0.0 copy-start.5
  11.4 2.2 %copy.22 = bf16[2,16,132,96]{3,2,0,1:T(8,128)(2,1)} copy(bf16[2,16,132,96]{2,1,3,0:T(8,128)(2,1)S(1)} %reshape.50) | data formatting | bytes 1622016 | tf_op jit(solution)/shard_map/reshape | solution.py:373
  13.6 39.5 %shard_map.177 = (bf16[16,2,132,96]{3,2,1,0:T(8,128)(2,1)}, f32[16,8,1,128]{3,2,1,0:T(1,128)}) custom-call(bf16[16,2,132,96]{3,2,1,0:T(8,128)(2,1)} %bitcast.25, f32[1,128]{1,0:T(1,128)} %pad.10.small), custom_call_target="tpu_custom_call" | custom-call | tf_op jit(solution)/shard_map/pallas_call | solution.py:258
  53.0 1.6 %reduce_sum.29 = f32[]{:T(128)} reduce(f32[16,8,1,128]{3,2,1,0:T(1,128)} %get-tuple-element.20, f32[]{:T(128)} %constant.5.clone.1), dimensions={0,1,2,3}, to_apply=%region_2.3 | reduce | flops 16383 | bytes 65544 | tf_op jit(solution)/shard_map/reduce_sum | solution.py:375
  55.3 0.0 copy-done
  55.3 0.0 copy-done.1
  55.3 0.0 copy-done.2
  55.3 0.0 copy-done.3
  55.3 0.0 copy-done.5
  55.4 0.6 multiply_add_fusion
  55.9 0.0 copy-start.4
  56.0 0.1 reshape.47
  56.0 0.5 pad_convert_fusion.small
  56.6 7.7 %shard_map.178 = (bf16[16,2,132,96]{3,2,1,0:T(8,128)(2,1)}, f32[132,2,1536]{2,1,0:T(2,128)}, f32[132,2,1536]{2,1,0:T(2,128)}, f32[132,2,1536]{2,1,0:T(2,128)}) custom-call(bf16[16,2,132,96]{3,2,1,0:T(8,128)(2,1)} %get-tuple-element.19.pieces, f32[1,1]{1,0:T(1,128)} %bitcast.2.scale, f32[132,2,1536]{2,1,0:T(2,128)} %bitcast.26, f32[132,2,1536]{2,1,0:T(2,128)} %bitcast.27, ...), custom_call_target="tpu_custom_call" | custom-call | tf_op jit(solution)/shard_map/pallas_call | solution.py:342
  64.3 0.0 copy-done.4
  64.3 46.8 %shard_map.179 = (bf16[16,2,132,96]{3,2,1,0:T(8,128)(2,1)}, bf16[16,2,132,96]{3,2,1,0:T(8,128)(2,1)}, f32[16,8,1,128]{3,2,1,0:T(1,128)}) custom-call(bf16[16,2,132,96]{3,2,1,0:T(8,128)(2,1)} %get-tuple-element.21.wire, f32[1,128]{1,0:T(1,128)} %pad_convert_fusion.small), custom_call_target="tpu_custom_call" | custom-call | tf_op jit(solution)/shard_map/pallas_call | solution.py:258
  111.1 0.9 convert.7
  112.0 0.1 copy.24
  112.1 0.1 copy.25
  112.2 0.7 convert_element_type.30
  113.0 3.2 %copy.29 = bf16[2,16,132,96]{2,1,3,0:T(8,128)(2,1)S(1)} copy(bf16[2,16,132,96]{3,2,0,1:T(8,128)(2,1)} %bitcast.31) | data formatting | bytes 1622016
  116.2 2.9 %reshape.51 = bf16[2,2112,96]{1,2,0:T(8,128)(2,1)} reshape(bf16[2,16,132,96]{2,1,3,0:T(8,128)(2,1)S(1)} %copy.29) | data formatting | bytes 1622016
  119.1 4.0 %shard_map.180 = f32[132,2,1536]{2,1,0:T(2,128)} custom-call(bf16[16,2,132,96]{3,2,1,0:T(8,128)(2,1)} %get-tuple-element.26.pieces, f32[132,2,1536]{2,1,0:T(2,128)} %bitcast.29), custom_call_target="tpu_custom_call" | custom-call | tf_op jit(solution)/shard_map/pallas_call | solution.py:342
  (2 shorter events, 0.0 us)
Async XLA Ops:
  11.3 44.0 %copy-start = (f32[2,24]{1,0:T(2,128)S(1)}, f32[2,24]{1,0:T(2,128)}, u32[]{:S(2)}) copy-start(f32[2,24]{1,0:T(2,128)} %param.19) | copy-start | bytes 580
  11.3 44.0 %copy-start.1 = (f32[2,24]{1,0:T(2,128)S(1)}, f32[2,24]{1,0:T(2,128)}, u32[]{:S(2)}) copy-start(f32[2,24]{1,0:T(2,128)} %param.16) | copy-start | bytes 580
  11.3 44.0 %copy-start.2 = (f32[2,24]{1,0:T(2,128)S(1)}, f32[2,24]{1,0:T(2,128)}, u32[]{:S(2)}) copy-start(f32[2,24]{1,0:T(2,128)} %param.17) | copy-start | bytes 580
  11.3 44.0 %copy-start.3 = (f32[2,24]{1,0:T(2,128)S(1)}, f32[2,24]{1,0:T(2,128)}, u32[]{:S(2)}) copy-start(f32[2,24]{1,0:T(2,128)} %param.18) | copy-start | bytes 580
  11.4 44.0 %copy-start.5 = (bf16[2,24]{1,0:T(2,128)(2,1)S(1)}, bf16[2,24]{1,0:T(2,128)(2,1)}, u32[]{:S(2)}) copy-start(bf16[2,24]{1,0:T(2,128)(2,1)} %param.15) | copy-start | bytes 292
  55.9 8.3 %copy-start.4 = (f32[2,24]{1,0:T(2,128)}, f32[2,24]{1,0:T(2,128)S(1)}, u32[]{:S(2)}) copy-start(f32[2,24]{1,0:T(2,128)S(1)} %get-tuple-element.39) | copy-start | bytes 580

commit v3 on v2

--- a/solution.py
+++ b/solution.py
@@ -1,3 +1,5 @@
+import functools
+
 import jax
 import jax.numpy as jnp
 from jax import lax
@@ -20,6 +22,7 @@
 MESH = pl.DeviceIdType.MESH
 FSDP = 16
 TENSOR = 8
+LANES = 128
 SPAN = 384
 
 
@@ -270,6 +273,41 @@
     )(wire, small)
 
 
+def total(x):
+    wide = x.astype(jnp.float32)
+    return jnp.sum(jnp.sum(wide * wide, axis=0, keepdims=True), axis=1, keepdims=True)
+
+
+def same(shape, shift):
+    i = lax.broadcasted_iota(jnp.int32, shape, 0)
+    j = lax.broadcasted_iota(jnp.int32, shape, 1)
+    return jnp.where(j == i + shift, 1.0, 0.0).astype(jnp.bfloat16)
+
+
+def turn(a, b):
+    return lax.dot_general(
+        a, b, (((1,), (1,)), ((), ())), preferred_element_type=jnp.float32
+    )
+
+
+def prepare_kernel(blocks, gains, wire, small):
+    layers, _, block_rows = blocks.shape
+    rows = wire.shape[2]
+    for k in range(FSDP):
+        start = rows * k // LANES * LANES
+        size = min(2 * LANES, block_rows - start)
+        chosen = same((rows, size), rows * k - start)
+        for layer in range(layers):
+            wire[k, layer] = turn(chosen, blocks[layer, :, pl.ds(start, size)]).astype(
+                wire.dtype
+            )
+    squares = total(gains[...])
+    for layer in range(layers):
+        squares += total(blocks[layer])
+    lane = lax.broadcasted_iota(jnp.int32, small.shape, 1)
+    small[...] = jnp.where(lane == 0, squares, 0.0)
+
+
 def joined(pieces, group, layer):
     return jnp.concatenate(
         [pieces[4 * group + i, layer].astype(jnp.float32) for i in range(4)], axis=1
@@ -288,18 +326,28 @@
 
 
 def update_kernel(
-    pieces, scale, master, first, second,
-    out_wire, master_out, first_out, second_out,
+    entries, pieces, sums, gain_grads, gain_master, gain_first, gain_second, gain_average,
+    master, first, second,
+    out_wire, gain_master_out, gain_first_out, gain_second_out, gain_average_out,
+    master_out, first_out, second_out,
     master_buf, first_buf, second_buf, *sems,
 ):
     cols = pieces.shape[3]
     refs = (master, first, second)
     outs = (master_out, first_out, second_out)
     bufs = (master_buf, first_buf, second_buf)
-    clip_scale = scale[0, 0]
     for step in STEPS:
         for i in range(3):
             part(refs[i], bufs[i], sems[i], *step, False).start()
+    squares = jnp.sum(jnp.sum(sums[...], axis=0, keepdims=True), axis=1, keepdims=True)
+    clip_scale = jnp.minimum(1.0, clip_level / jnp.sqrt(squares / entries + mean_epsilon))
+    gain_news = adam_step(
+        gain_grads[...], gain_master[...], gain_first[...], gain_second[...], clip_scale
+    )
+    gain_master_out[...], gain_first_out[...], gain_second_out[...] = gain_news
+    gain_average_out[...] = (
+        average_decay * gain_average[...] + (1.0 - average_decay) * gain_news[0]
+    )
     for layer, group in STEPS:
         span = slice(group * SPAN, (group + 1) * SPAN)
         grads = joined(pieces, group, layer)
@@ -318,7 +366,9 @@
             part(outs[i], bufs[i], sems[3 + i], *step, True).wait()
 
 
-def average_kernel(pieces, average, average_out, buf, sem, sem_out):
+def finish_kernel(
+    train, pieces, average, train_out, average_out, buf, sem, sem_out, stack
+):
     for step in STEPS:
         part(average, buf, sem, *step, False).start()
     for layer, group in STEPS:
@@ -329,6 +379,18 @@
             average_decay * buf[layer, :, span] + (1.0 - average_decay) * news
         )
         part(average_out, buf, sem_out, layer, group, True).start()
+    layers, cols, block_rows = train_out.shape
+    rows = train.shape[2]
+    unit = same((cols, cols), 0)
+    for layer in range(layers):
+        for k in range(FSDP):
+            stack[pl.ds(rows * k, rows), :] = train[k, layer].astype(jnp.float32)
+        for start in range(0, block_rows, 2 * LANES):
+            size = min(2 * LANES, block_rows - start)
+            here = pl.ds(start, size)
+            train_out[layer, :, here] = turn(
+                unit, stack[here, :].astype(jnp.bfloat16)
+            ).astype(train_out.dtype)
     for step in STEPS:
         part(average_out, buf, sem_out, *step, True).wait()
 
@@ -337,7 +399,7 @@
     return x.transpose(1, 0, 2)
 
 
-def plain(kernel, outputs, out_specs, operands, specs, states):
+def plain(kernel, outputs, out_specs, operands, specs, states, scratch=()):
     shape = (2, outputs[-1].shape[0], 4 * SPAN)
     return pl.pallas_call(
         kernel,
@@ -345,7 +407,8 @@
         in_specs=specs,
         out_specs=out_specs,
         scratch_shapes=[pltpu.VMEM(shape, jnp.float32)] * states
-        + [pltpu.SemaphoreType.DMA((2, 4))] * (2 * states),
+        + [pltpu.SemaphoreType.DMA((2, 4))] * (2 * states)
+        + list(scratch),
     )(*operands)
 
 
@@ -366,56 +429,62 @@
     width = block_cols * FSDP
     entries = (grad_blocks.size + gain_grads.size) * FSDP * TENSOR
 
-    wide = grad_blocks.astype(jnp.float32)
-    gain_wide = gain_grads.astype(jnp.float32)
-    squares = jnp.sum(wide * wide) + jnp.sum(gain_wide * gain_wide)
-    small = jnp.pad(squares.reshape(1, 1), ((0, 0), (0, 127)))
-    wire = grad_blocks.reshape(layers, FSDP, rows, block_cols).transpose(1, 0, 2, 3)
+    vmem = pl.BlockSpec(memory_space=pltpu.VMEM)
+    far = pl.BlockSpec(memory_space=pl.ANY)
+    one_row = jax.ShapeDtypeStruct((1, LANES), jnp.float32)
+    wire_shape = jax.ShapeDtypeStruct((FSDP, layers, rows, block_cols), grad_blocks.dtype)
+    flat = jax.ShapeDtypeStruct((rows, layers, width), jnp.float32)
+    gain = jax.ShapeDtypeStruct(gain_master.shape, jnp.float32)
+
+    wire, small = pl.pallas_call(
+        prepare_kernel,
+        out_shape=[wire_shape, one_row],
+        in_specs=[vmem] * 2,
+        out_specs=[vmem] * 2,
+    )(grad_blocks.transpose(0, 2, 1), gain_grads)
     pieces, sums = exchange(gather_kernel, wire, small, 1, 2, 0)
-    total_squares = jnp.sum(sums)
-    clip_scale = jnp.minimum(1.0, clip_level / jnp.sqrt(total_squares / entries + mean_epsilon))
-
-    vmem = pl.BlockSpec(memory_space=pltpu.VMEM)
-    smem = pl.BlockSpec(memory_space=pltpu.SMEM)
-    far = pl.BlockSpec(memory_space=pl.ANY)
-    flat = jax.ShapeDtypeStruct((rows, layers, width), jnp.float32)
-    wire_out = jax.ShapeDtypeStruct(wire.shape, wire.dtype)
-    out_wire, master_next, first_next, second_next = plain(
-        update_kernel,
-        [wire_out, flat, flat, flat],
-        [vmem, far, far, far],
+
+    (
+        out_wire,
+        master_gains,
+        first_gains,
+        second_gains,
+        average_gains,
+        master_next,
+        first_next,
+        second_next,
+    ) = plain(
+        functools.partial(update_kernel, entries),
+        [wire_shape] + [gain] * 4 + [flat] * 3,
+        [vmem] * 5 + [far] * 3,
         (
             pieces,
-            clip_scale.reshape(1, 1),
+            sums.reshape(FSDP * TENSOR, LANES),
+            gain_grads,
+            gain_master,
+            gain_first,
+            gain_second,
+            gain_average,
             turned(master_shard),
             turned(first_moment),
             turned(second_moment),
         ),
-        [vmem, smem, far, far, far],
+        [vmem] * 7 + [far] * 3,
         3,
     )
-    master_gains, first_gains, second_gains = adam_step(
-        gain_grads, gain_master, gain_first, gain_second, clip_scale
-    )
-    average_gains = average_decay * gain_average + (1.0 - average_decay) * master_gains
-
-    gain_count = gain_grads.size
-    gain_cols = gain_grads.shape[1]
-    gain_small = jnp.pad(
-        master_gains.astype(jnp.bfloat16).astype(jnp.float32).reshape(1, gain_count),
-        ((0, 0), (0, 128 - gain_count)),
-    )
-    train, averages, gains = exchange(spread_kernel, out_wire, gain_small, 2, 3, 1)
-    train_weights = train.transpose(1, 0, 2, 3).reshape(layers, block_rows, block_cols)
-    (average_next,) = plain(
-        average_kernel, [flat], [far], (averages, turned(average_shard)), [vmem, far], 1
-    )
+    train, averages, gains = exchange(spread_kernel, out_wire, master_gains, 2, 3, 1)
+    train_turned, average_next = plain(
+        finish_kernel,
+        [jax.ShapeDtypeStruct((layers, block_cols, block_rows), jnp.bfloat16), flat],
+        [vmem, far],
+        (train, averages, turned(average_shard)),
+        [vmem, vmem, far],
+        1,
+        [pltpu.VMEM((block_rows, block_cols), jnp.float32)],
+    )
+    train_weights = train_turned.transpose(0, 2, 1)
     gain_weights = (
-        gains.reshape(FSDP * TENSOR, 128)[:, :gain_count]
-        .reshape(FSDP * TENSOR, layers, gain_cols)
-        .transpose(1, 0, 2)
-        .reshape(layers, FSDP * TENSOR * gain_cols)
-        .astype(jnp.bfloat16)
+        gains.astype(jnp.bfloat16).transpose(2, 0, 1, 3).reshape(layers, -1)
     )
     return (
         train_weights,

time: 124 us -> 105 us (0.85)
  local copies, waits for them, and re-layouts: 15.3 us -> 0.74 us
  other arithmetic: 7.03 us -> 0.95 us
  Pallas kernels: 98 us -> 102 us
  between operations: 2.79 us -> 0.68 us
    reshape x3 -> x1, local copies, waits for them, and re-layouts: 7.67 us -> 0.73 us  [on_device(): gains.astype(jnp.bfloat16).transpose(2, 0, 1, 3).reshape(layers, -1)]
    unnamed x15 -> x0, local copies, waits for them, and re-layouts: 6.19 us -> none
    reduce_sum x3 -> x0, other arithmetic: 5.03 us -> none  [the longest x2 3.45 us: on_device(): squares = jnp.sum(wide * wide) + jnp.sum(gain_wide * gain_wide)]
    pallas_call x0 -> x1, Pallas kernels: none -> 2.92 us  [on_device(): pl.pallas_call(prepare_kernel, out_shape=[wire_shape, one_row], in_specs=...]
    pallas_call x2, Pallas kernels: 11.7 us -> 13.1 us  [plain(): pl.pallas_call(kernel, out_shape=outputs, in_specs=specs, out_specs=out_s...]
where the time goes in v3:
time: 105 us
  Pallas kernels  102 us (97%)
    pallas_call x2, Pallas kernels, exchange(): pl.pallas_call(kernel, out_shape=[pieces] * outputs + [jax.ShapeDtypeStru...  86.4 us
    pallas_call x2, Pallas kernels, plain(): pl.pallas_call(kernel, out_shape=outputs, in_specs=specs, out_specs=out_s...  13.1 us
    pallas_call x1, Pallas kernels, on_device(): pl.pallas_call(prepare_kernel, out_shape=[wire_shape, one_row], in_specs=...  2.92 us

profile of v3, /device:TPU:6, one launch (start us, length us, event | category | flops | bytes accessed | tf_op | source)
XLA Modules:
  0.0 104.8 jit_solution(11655610806142814096)
XLA Ops:
  0.6 2.9 %shard_map.177 = (bf16[16,2,132,96]{3,2,1,0:T(8,128)(2,1)}, f32[1,128]{1,0:T(1,128)}) custom-call(bf16[2,96,2112]{2,1,0:T(8,128)(2,1)} %bitcast.19, bf16[2,24]{1,0:T(2,128)(2,1)} %gain_grads.1), custom_call_target="tpu_custom_call" | custom-call | tf_op jit(solution)/shard_map/pallas_call | solution.py:439
  3.6 39.5 %shard_map.178 = (bf16[16,2,132,96]{3,2,1,0:T(8,128)(2,1)}, f32[16,8,1,128]{3,2,1,0:T(1,128)}) custom-call(bf16[16,2,132,96]{3,2,1,0:T(8,128)(2,1)} %get-tuple-element.27.wire, f32[1,128]{1,0:T(1,128)} %get-tuple-element.28.small), custom_call_target="tpu_custom_call" | custom-call | tf_op jit(solution)/shard_map/pallas_call | solution.py:261
  43.0 7.9 %shard_map.179 = (bf16[16,2,132,96]{3,2,1,0:T(8,128)(2,1)}, f32[2,24]{1,0:T(2,128)}, f32[2,24]{1,0:T(2,128)}, f32[2,24]{1,0:T(2,128)}, f32[2,24]{1,0:T(2,128)}, ...) custom-call(bf16[16,2,132,96]{3,2,1,0:T(8,128)(2,1)} %get-tuple-element.29.pieces, ...), custom_call_target="tpu_custom_call" | custom-call | tf_op jit(solution)/shard_map/pallas_call | solution.py:404
  50.9 46.9 %shard_map.180 = (bf16[16,2,132,96]{3,2,1,0:T(8,128)(2,1)}, bf16[16,2,132,96]{3,2,1,0:T(8,128)(2,1)}, f32[16,8,2,24]{3,2,1,0:T(2,128)}) custom-call(bf16[16,2,132,96]{3,2,1,0:T(8,128)(2,1)} %get-tuple-element.31.wire, f32[2,24]{1,0:T(2,128)} %get-tuple-element.23.small), custom_call_target="tpu_custom_call" | custom-call | tf_op jit(solution)/shard_map/pallas_call | solution.py:261
  97.8 1.0 convert_bitcast_fusion
  98.8 0.7 reshape.27
  99.5 5.2 %shard_map.181 = (bf16[2,96,2112]{2,1,0:T(8,128)(2,1)}, f32[132,2,1536]{2,1,0:T(2,128)}) custom-call(bf16[16,2,132,96]{3,2,1,0:T(8,128)(2,1)} %get-tuple-element.33.train, bf16[16,2,132,96]{3,2,1,0:T(8,128)(2,1)} %get-tuple-element.34.pieces, f32[132,2,1536]{2,1,0:T(2,128)} %bitcast.18), custom_call_target="tpu_custom_call" | custom-call | tf_op jit(solution)/shard_map/pallas_call | solution.py:404
  (1 shorter events, 0.0 us)

commit v4 on v3

--- a/solution.py
+++ b/solution.py
@@ -159,7 +159,6 @@
     sems = (rs, rr, cs, cr)
     enter(f, t)
     small_first(f, t, small, sums, sems)
-    small_second(f, t, small, sums, sems)
 
     def stage_a(n):
         i, half = n // 2, lax.rem(n + f // TENSOR, 2)
@@ -178,6 +177,8 @@
     @pl.loop(0, FSDP)
     def _(n):
         send(*stage_a(n))
+
+    small_second(f, t, small, sums, sems)
 
     @pl.loop(0, FSDP)
     def _(n):
@@ -290,17 +291,37 @@
     )
 
 
+def put_tails(wire, k, tails):
+    count, cols = tails.shape
+    full = jnp.concatenate([tails, jnp.zeros((count, LANES - cols), jnp.float32)], axis=1)
+    wire[k, pl.ds(wire.shape[1] - count, count), :] = full.astype(wire.dtype)
+
+
+def unpack(pieces, k, layer, cols, unit):
+    rest = pieces.shape[1] // 2 - cols
+    head = turn(unit, pieces[k, pl.ds(layer * cols, cols), :])
+    tails = pieces[k, pl.ds(2 * cols, 2 * rest), :].astype(jnp.float32)
+    return jnp.concatenate([head, tails[layer * rest : (layer + 1) * rest, :cols]], axis=0)
+
+
 def prepare_kernel(blocks, gains, wire, small):
-    layers, _, block_rows = blocks.shape
-    rows = wire.shape[2]
+    layers, cols, block_rows = blocks.shape
+    rows = block_rows // FSDP
+    rest = rows - LANES
     for k in range(FSDP):
         start = rows * k // LANES * LANES
         size = min(2 * LANES, block_rows - start)
-        chosen = same((rows, size), rows * k - start)
+        shift = rows * k - start
+        chosen = same((LANES, size), shift)
+        tails = jnp.zeros((layers * rest, cols), jnp.float32)
         for layer in range(layers):
-            wire[k, layer] = turn(chosen, blocks[layer, :, pl.ds(start, size)]).astype(
-                wire.dtype
-            )
+            window = blocks[layer, :, pl.ds(start, size)]
+            wire[k, pl.ds(layer * cols, cols), :] = turn(window, chosen).astype(wire.dtype)
+            i = lax.broadcasted_iota(jnp.int32, (layers * rest, size), 0) - layer * rest
+            j = lax.broadcasted_iota(jnp.int32, (layers * rest, size), 1) - shift - LANES
+            hit = (i == j) & (i >= 0) & (i < rest)
+            tails += turn(jnp.where(hit, 1.0, 0.0).astype(window.dtype), window)
+        put_tails(wire, k, tails)
     squares = total(gains[...])
     for layer in range(layers):
         squares += total(blocks[layer])
@@ -308,9 +329,9 @@
     small[...] = jnp.where(lane == 0, squares, 0.0)
 
 
-def joined(pieces, group, layer):
+def joined(pieces, group, layer, unit):
     return jnp.concatenate(
-        [pieces[4 * group + i, layer].astype(jnp.float32) for i in range(4)], axis=1
+        [unpack(pieces, 4 * group + i, layer, SPAN // 4, unit) for i in range(4)], axis=1
     )
 
 
@@ -322,7 +343,7 @@
     return pltpu.make_async_copy(there, here, sem.at[layer, group])
 
 
-STEPS = [(layer, group) for layer in range(2) for group in range(4)]
+STEPS = [(layer, group) for group in range(4) for layer in range(2)]
 
 
 def update_kernel(
@@ -332,7 +353,10 @@
     master_out, first_out, second_out,
     master_buf, first_buf, second_buf, *sems,
 ):
-    cols = pieces.shape[3]
+    cols = SPAN // 4
+    unit = same((LANES, LANES), 0)
+    unit_cols = same((cols, cols), 0)
+    tails = {}
     refs = (master, first, second)
     outs = (master_out, first_out, second_out)
     bufs = (master_buf, first_buf, second_buf)
@@ -350,7 +374,7 @@
     )
     for layer, group in STEPS:
         span = slice(group * SPAN, (group + 1) * SPAN)
-        grads = joined(pieces, group, layer)
+        grads = joined(pieces, group, layer, unit)
         for i in range(3):
             part(refs[i], bufs[i], sems[i], layer, group, False).wait()
         news = adam_step(grads, *[buf[layer, :, span] for buf in bufs], clip_scale)
@@ -358,9 +382,15 @@
             bufs[i][layer, :, span] = news[i]
             part(outs[i], bufs[i], sems[3 + i], layer, group, True).start()
         for i in range(4):
-            out_wire[4 * group + i, layer] = news[0][:, i * cols : (i + 1) * cols].astype(
-                out_wire.dtype
-            )
+            piece = news[0][:, i * cols : (i + 1) * cols]
+            out_wire[4 * group + i, pl.ds(layer * cols, cols), :] = turn(
+                unit_cols, piece[:LANES].astype(out_wire.dtype)
+            ).astype(out_wire.dtype)
+            tails[i, layer] = piece[LANES:]
+        if layer == 1:
+            for i in range(4):
+                both = jnp.concatenate([tails[i, 0], tails[i, 1]], axis=0)
+                put_tails(out_wire, 4 * group + i, both)
     for step in STEPS:
         for i in range(3):
             part(outs[i], bufs[i], sems[3 + i], *step, True).wait()
@@ -371,25 +401,26 @@
 ):
     for step in STEPS:
         part(average, buf, sem, *step, False).start()
+    unit = same((LANES, LANES), 0)
     for layer, group in STEPS:
         span = slice(group * SPAN, (group + 1) * SPAN)
-        news = joined(pieces, group, layer)
+        news = joined(pieces, group, layer, unit)
         part(average, buf, sem, layer, group, False).wait()
         buf[layer, :, span] = (
             average_decay * buf[layer, :, span] + (1.0 - average_decay) * news
         )
         part(average_out, buf, sem_out, layer, group, True).start()
     layers, cols, block_rows = train_out.shape
-    rows = train.shape[2]
-    unit = same((cols, cols), 0)
+    rows = block_rows // FSDP
+    unit_cols = same((cols, cols), 0)
     for layer in range(layers):
         for k in range(FSDP):
-            stack[pl.ds(rows * k, rows), :] = train[k, layer].astype(jnp.float32)
+            stack[pl.ds(rows * k, rows), :] = unpack(train, k, layer, cols, unit)
         for start in range(0, block_rows, 2 * LANES):
             size = min(2 * LANES, block_rows - start)
             here = pl.ds(start, size)
             train_out[layer, :, here] = turn(
-                unit, stack[here, :].astype(jnp.bfloat16)
+                unit_cols, stack[here, :].astype(jnp.bfloat16)
             ).astype(train_out.dtype)
     for step in STEPS:
         part(average_out, buf, sem_out, *step, True).wait()
@@ -432,7 +463,8 @@
     vmem = pl.BlockSpec(memory_space=pltpu.VMEM)
     far = pl.BlockSpec(memory_space=pl.ANY)
     one_row = jax.ShapeDtypeStruct((1, LANES), jnp.float32)
-    wire_shape = jax.ShapeDtypeStruct((FSDP, layers, rows, block_cols), grad_blocks.dtype)
+    dense = layers * (block_cols + rows - LANES)
+    wire_shape = jax.ShapeDtypeStruct((FSDP, dense, LANES), grad_blocks.dtype)
     flat = jax.ShapeDtypeStruct((rows, layers, width), jnp.float32)
     gain = jax.ShapeDtypeStruct(gain_master.shape, jnp.float32)
 

time: 105 us -> 90.9 us (0.87)
  Pallas kernels: 102 us -> 88.3 us
    pallas_call x2, Pallas kernels: 86.4 us -> 69.4 us  [exchange(): pl.pallas_call(kernel, out_shape=[pieces] * outputs + [jax.ShapeDtypeStru...]
    pallas_call x2, Pallas kernels: 13.1 us -> 15.7 us  [plain(): pl.pallas_call(kernel, out_shape=outputs, in_specs=specs, out_specs=out_s...]
where the time goes in v4:
time: 90.9 us; the launch traced here: 90.7 us
  Pallas kernels  88.3 us (97%)
  other arithmetic  0.95 us (1%)
    pallas_call x2, Pallas kernels, exchange(): pl.pallas_call(kernel, out_shape=[pieces] * outputs + [jax.ShapeDtypeStru...  69.4 us
    pallas_call x2, Pallas kernels, plain(): pl.pallas_call(kernel, out_shape=outputs, in_specs=specs, out_specs=out_s...  15.7 us
    pallas_call x1, Pallas kernels, on_device(): pl.pallas_call(prepare_kernel, out_shape=[wire_shape, one_row], in_specs=...  3.18 us

profile of v4, /device:TPU:6, one launch (start us, length us, event | category | flops | bytes accessed | tf_op | source)
XLA Modules:
  0.0 90.7 jit_solution(3806908781450508272)
XLA Ops:
  0.6 3.2 %shard_map.177 = (bf16[16,200,128]{2,1,0:T(8,128)(2,1)}, f32[1,128]{1,0:T(1,128)}) custom-call(bf16[2,96,2112]{2,1,0:T(8,128)(2,1)} %bitcast.19, bf16[2,24]{1,0:T(2,128)(2,1)} %gain_grads.1), custom_call_target="tpu_custom_call" | custom-call | tf_op jit(solution)/shard_map/pallas_call | solution.py:471
  3.8 28.2 %shard_map.178 = (bf16[16,200,128]{2,1,0:T(8,128)(2,1)}, f32[16,8,1,128]{3,2,1,0:T(1,128)}) custom-call(bf16[16,200,128]{2,1,0:T(8,128)(2,1)} %get-tuple-element.27.wire, f32[1,128]{1,0:T(1,128)} %get-tuple-element.28.small), custom_call_target="tpu_custom_call" | custom-call | tf_op jit(solution)/shard_map/pallas_call | solution.py:262
  32.0 8.9 %shard_map.179 = (bf16[16,200,128]{2,1,0:T(8,128)(2,1)}, f32[2,24]{1,0:T(2,128)}, f32[2,24]{1,0:T(2,128)}, f32[2,24]{1,0:T(2,128)}, f32[2,24]{1,0:T(2,128)}, /*i...) custom-call(bf16[16,200,128]{2,1,0:T(8,128)(2,1)} %get-tuple-element.29.pieces, ...), custom_call_target="tpu_custom_call" | custom-call | tf_op jit(solution)/shard_map/pallas_call | solution.py:435
  41.0 41.2 %shard_map.180 = (bf16[16,200,128]{2,1,0:T(8,128)(2,1)}, bf16[16,200,128]{2,1,0:T(8,128)(2,1)}, f32[16,8,2,24]{3,2,1,0:T(2,128)}) custom-call(bf16[16,200,128]{2,1,0:T(8,128)(2,1)} %get-tuple-element.31.wire, f32[2,24]{1,0:T(2,128)} %get-tuple-element.23.small), custom_call_target="tpu_custom_call" | custom-call | tf_op jit(solution)/shard_map/pallas_call | solution.py:262
  82.2 1.0 %convert_bitcast_fusion = bf16[2,16,8,24]{3,0,2,1:T(2,128)(2,1)S(1)} fusion(f32[16,8,2,24]{3,2,1,0:T(2,128)} %get-tuple-element.40), kind=kLoop, calls=%fused_computation | loop fusion | flops 6144 | bytes 36864 | tf_op jit(solution)/shard_map/transpose | solution.py:519
  83.2 0.7 reshape.27
  83.9 6.7 %shard_map.181 = (bf16[2,96,2112]{2,1,0:T(8,128)(2,1)}, f32[132,2,1536]{2,1,0:T(2,128)}) custom-call(bf16[16,200,128]{2,1,0:T(8,128)(2,1)} %get-tuple-element.33.train, bf16[16,200,128]{2,1,0:T(8,128)(2,1)} %get-tuple-element.34.pieces, f32[132,2,1536]{2,1,0:T(2,128)} %bitcast.18), custom_call_target="tpu_custom_call" | custom-call | tf_op jit(solution)/shard_map/pallas_call | solution.py:435
  (1 shorter events, 0.0 us)

commit v5 on v4

--- a/solution.py
+++ b/solution.py
@@ -40,7 +40,7 @@
     return (master_new, first_new, second_new)
 
 
-def enter(f, t):
+def enter(f, t, sources=None):
     barrier = pltpu.get_barrier_semaphore()
 
     @pl.loop(1, TENSOR)
@@ -55,7 +55,21 @@
             barrier, inc=1, device_id=(lax.rem(f + i, FSDP), t), device_id_type=MESH
         )
 
-    pl.semaphore_wait(barrier, TENSOR + FSDP - 2)
+    peers = TENSOR + FSDP - 2
+    if sources is not None:
+        peers += FSDP - (f // 2 == t).astype(jnp.int32)
+
+        @pl.loop(0, FSDP)
+        def _(i):
+            source_f, source_t = sources(i)
+
+            @pl.when(jnp.logical_not((source_f == f) & (source_t == t)))
+            def _():
+                pl.semaphore_signal(
+                    barrier, inc=1, device_id=(source_f, source_t), device_id_type=MESH
+                )
+
+    pl.semaphore_wait(barrier, peers)
 
 
 def remote(source, target, send_sem, recv_sem, device):
@@ -151,74 +165,51 @@
         col_copy(i).wait_send()
 
 
-def gather_kernel(
-    wire, small, out, sums, mid, send_a, recv_a, send_b, recv_b, rs, rr, cs, cr
+def gather_kernel(wire, small, out, sums, send_a, recv_a, rs, rr, cs, cr):
+    f = lax.axis_index("fsdp")
+    t = lax.axis_index("tensor")
+    sems = (rs, rr, cs, cr)
+    enter(f, t, lambda i: (i, f // 2))
+    small_first(f, t, small, sums, sems)
+    small_second(f, t, small, sums, sems)
+
+    def stage_a(n):
+        half = lax.rem(n + f // TENSOR, 2)
+        to = lax.rem(t + n // 2 + f, TENSOR)
+        k = half * TENSOR + to
+        m = 2 * t + half
+        is_own = (to == t) & (m == f)
+        return (wire.at[k], out.at[f], send_a.at[k], recv_a.at[f], (m, to), is_own)
+
+    @pl.loop(0, FSDP)
+    def _(n):
+        send(*stage_a(n))
+
+    @pl.loop(0, FSDP)
+    def _(n):
+        arrived(out.at[n], recv_a.at[n])
+
+    small_done(f, t, small, sums, sems)
+
+    @pl.loop(0, FSDP)
+    def _(n):
+        sent(*stage_a(n))
+
+
+def spread_kernel(
+    wire, small, train, average, gains, send_a, recv_a, send_c, recv_c, rs, rr, cs, cr
 ):
     f = lax.axis_index("fsdp")
     t = lax.axis_index("tensor")
     sems = (rs, rr, cs, cr)
-    enter(f, t)
-    small_first(f, t, small, sums, sems)
-
-    def stage_a(n):
-        i, half = n // 2, lax.rem(n + f // TENSOR, 2)
-        to = lax.rem(t + i + f, TENSOR)
-        k = half * TENSOR + to
-        slot = 2 * t + half
-        return (
-            wire.at[k], mid.at[slot], send_a.at[k], recv_a.at[slot], (f, to), to == t,
-        )
-
-    def stage_b(n):
-        i, half = n // 2, lax.rem(n + f // TENSOR, 2)
-        m = 2 * lax.rem(t - i - f + 4 * TENSOR, TENSOR) + half
-        return m, (mid.at[m], out.at[f], send_b.at[m], recv_b.at[f], (m, t), m == f)
-
-    @pl.loop(0, FSDP)
-    def _(n):
-        send(*stage_a(n))
-
-    small_second(f, t, small, sums, sems)
-
-    @pl.loop(0, FSDP)
-    def _(n):
-        m, copy = stage_b(n)
-        arrived(mid.at[m], recv_a.at[m])
-        send(*copy)
-
-    @pl.loop(0, FSDP)
-    def _(n):
-        arrived(out.at[n], recv_b.at[n])
-
-    small_done(f, t, small, sums, sems)
-
-    @pl.loop(0, FSDP)
-    def _(n):
-        sent(*stage_a(n))
-        sent(*stage_b(n)[1])
-
-
-def spread_kernel(
-    wire, small, train, average, gains, mid,
-    send_a, recv_a, send_b, recv_b, send_c, recv_c, rs, rr, cs, cr,
-):
-    f = lax.axis_index("fsdp")
-    t = lax.axis_index("tensor")
-    sems = (rs, rr, cs, cr)
-    enter(f, t)
+    enter(f, t, lambda i: (2 * t + i // TENSOR, lax.rem(i, TENSOR)))
     small_first(f, t, small, gains, sems)
 
     def stage_a(n):
         j = lax.rem(f + n + 2 * t, FSDP)
-        return (wire.at[j], mid.at[f], send_a.at[j], recv_a.at[f], (j, t), j == f)
-
-    def stage_b(n):
-        source = lax.rem(f - n - 2 * t + 2 * FSDP, FSDP)
-        to = source // 2
-        k = lax.rem(source, 2) * TENSOR + t
-        return source, (
-            mid.at[source], train.at[k], send_b.at[source], recv_b.at[k], (f, to), to == t,
-        )
+        k = lax.rem(f, 2) * TENSOR + t
+        is_own = (j == f) & (f // 2 == t)
+        return (wire.at[j], train.at[k], send_a.at[j], recv_a.at[k], (j, f // 2), is_own)
 
     def stage_c(n):
         k = lax.rem(n, 2) * TENSOR + lax.rem(n // 2 + f + t, TENSOR)
@@ -228,20 +219,14 @@
     def _(n):
         send(*stage_a(n))
 
-    @pl.loop(0, FSDP)
-    def _(n):
-        source, copy = stage_b(n)
-        arrived(mid.at[source], recv_a.at[source])
+    small_second(f, t, small, gains, sems)
+
+    @pl.loop(0, FSDP)
+    def _(n):
+        k, copy = stage_c(n)
+        arrived(train.at[k], recv_a.at[k])
         send(*copy)
 
-    small_second(f, t, small, gains, sems)
-
-    @pl.loop(0, FSDP)
-    def _(n):
-        k, copy = stage_c(n)
-        arrived(train.at[k], recv_b.at[k])
-        send(*copy)
-
     @pl.loop(0, FSDP)
     def _(n):
         arrived(average.at[n], recv_c.at[n])
@@ -251,11 +236,10 @@
     @pl.loop(0, FSDP)
     def _(n):
         sent(*stage_a(n))
-        sent(*stage_b(n)[1])
         sent(*stage_c(n)[1])
 
 
-def exchange(kernel, wire, small, outputs, stages, collective_id):
+def exchange(kernel, wire, small, outputs, relays, stages, collective_id):
     vmem = pl.BlockSpec(memory_space=pltpu.VMEM)
     pieces = jax.ShapeDtypeStruct(wire.shape, wire.dtype)
     dma = pltpu.SemaphoreType.DMA
@@ -265,7 +249,7 @@
         + [jax.ShapeDtypeStruct((FSDP, TENSOR) + small.shape, small.dtype)],
         in_specs=[vmem] * 2,
         out_specs=[vmem] * (outputs + 1),
-        scratch_shapes=[pltpu.VMEM(wire.shape, wire.dtype)]
+        scratch_shapes=[pltpu.VMEM(wire.shape, wire.dtype)] * relays
         + [dma((FSDP,))] * (2 * stages)
         + [dma((TENSOR,)), dma((TENSOR,)), dma((FSDP,)), dma((FSDP,))],
         compiler_params=pltpu.CompilerParams(
@@ -474,7 +458,7 @@
         in_specs=[vmem] * 2,
         out_specs=[vmem] * 2,
     )(grad_blocks.transpose(0, 2, 1), gain_grads)
-    pieces, sums = exchange(gather_kernel, wire, small, 1, 2, 0)
+    pieces, sums = exchange(gather_kernel, wire, small, 1, 0, 1, 0)
 
     (
         out_wire,
@@ -504,7 +488,7 @@
         [vmem] * 7 + [far] * 3,
         3,
     )
-    train, averages, gains = exchange(spread_kernel, out_wire, master_gains, 2, 3, 1)
+    train, averages, gains = exchange(spread_kernel, out_wire, master_gains, 2, 0, 2, 1)
     train_turned, average_next = plain(
         finish_kernel,
         [jax.ShapeDtypeStruct((layers, block_cols, block_rows), jnp.bfloat16), flat],

time: 90.9 us -> 114 us (1.25)
  the two profiles are of different devices: /device:TPU:6 before, /device:TPU:5 now
where the time goes in v5:
time: 114 us
  Pallas kernels  111 us (97%)
    pallas_call x2, Pallas kernels, exchange(): pl.pallas_call(kernel, out_shape=[pieces] * outputs + [jax.ShapeDtypeStru...  92.3 us
    pallas_call x2, Pallas kernels, plain(): pl.pallas_call(kernel, out_shape=outputs, in_specs=specs, out_specs=out_s...  15.7 us
    pallas_call x1, Pallas kernels, on_device(): pl.pallas_call(prepare_kernel, out_shape=[wire_shape, one_row], in_specs=...  3.18 us

profile of v5, /device:TPU:5, one launch (start us, length us, event | category | flops | bytes accessed | tf_op | source)
XLA Modules:
  0.0 113.6 jit_solution(2560641474570127200)
XLA Ops:
  0.6 3.2 %shard_map.177 = (bf16[16,200,128]{2,1,0:T(8,128)(2,1)}, f32[1,128]{1,0:T(1,128)}) custom-call(bf16[2,96,2112]{2,1,0:T(8,128)(2,1)} %bitcast.19, bf16[2,24]{1,0:T(2,128)(2,1)} %gain_grads.1), custom_call_target="tpu_custom_call" | custom-call | tf_op jit(solution)/shard_map/pallas_call | solution.py:455
  3.8 31.0 %shard_map.178 = (bf16[16,200,128]{2,1,0:T(8,128)(2,1)}, f32[16,8,1,128]{3,2,1,0:T(1,128)}) custom-call(bf16[16,200,128]{2,1,0:T(8,128)(2,1)} %get-tuple-element.27.wire, f32[1,128]{1,0:T(1,128)} %get-tuple-element.28.small), custom_call_target="tpu_custom_call" | custom-call | tf_op jit(solution)/shard_map/pallas_call | solution.py:246
  34.9 8.9 %shard_map.179 = (bf16[16,200,128]{2,1,0:T(8,128)(2,1)}, f32[2,24]{1,0:T(2,128)}, f32[2,24]{1,0:T(2,128)}, f32[2,24]{1,0:T(2,128)}, f32[2,24]{1,0:T(2,128)}, /*i...) custom-call(bf16[16,200,128]{2,1,0:T(8,128)(2,1)} %get-tuple-element.29.pieces, ...), custom_call_target="tpu_custom_call" | custom-call | tf_op jit(solution)/shard_map/pallas_call | solution.py:419
  43.8 61.3 %shard_map.180 = (bf16[16,200,128]{2,1,0:T(8,128)(2,1)}, bf16[16,200,128]{2,1,0:T(8,128)(2,1)}, f32[16,8,2,24]{3,2,1,0:T(2,128)}) custom-call(bf16[16,200,128]{2,1,0:T(8,128)(2,1)} %get-tuple-element.31.wire, f32[2,24]{1,0:T(2,128)} %get-tuple-element.23.small), custom_call_target="tpu_custom_call" | custom-call | tf_op jit(solution)/shard_map/pallas_call | solution.py:246
  105.1 1.0 convert_bitcast_fusion
  106.1 0.7 reshape.27
  106.8 6.7 %shard_map.181 = (bf16[2,96,2112]{2,1,0:T(8,128)(2,1)}, f32[132,2,1536]{2,1,0:T(2,128)}) custom-call(bf16[16,200,128]{2,1,0:T(8,128)(2,1)} %get-tuple-element.33.train, bf16[16,200,128]{2,1,0:T(8,128)(2,1)} %get-tuple-element.34.pieces, f32[132,2,1536]{2,1,0:T(2,128)} %bitcast.18), custom_call_target="tpu_custom_call" | custom-call | tf_op jit(solution)/shard_map/pallas_call | solution.py:419
  (1 shorter events, 0.0 us)

commit v6 on v5

--- a/solution.py
+++ b/solution.py
@@ -171,7 +171,6 @@
     sems = (rs, rr, cs, cr)
     enter(f, t, lambda i: (i, f // 2))
     small_first(f, t, small, sums, sems)
-    small_second(f, t, small, sums, sems)
 
     def stage_a(n):
         half = lax.rem(n + f // TENSOR, 2)
@@ -181,10 +180,16 @@
         is_own = (to == t) & (m == f)
         return (wire.at[k], out.at[f], send_a.at[k], recv_a.at[f], (m, to), is_own)
 
-    @pl.loop(0, FSDP)
+    @pl.loop(0, 6)
     def _(n):
         send(*stage_a(n))
 
+    small_second(f, t, small, sums, sems)
+
+    @pl.loop(6, FSDP)
+    def _(n):
+        send(*stage_a(n))
+
     @pl.loop(0, FSDP)
     def _(n):
         arrived(out.at[n], recv_a.at[n])
@@ -197,34 +202,48 @@
 
 
 def spread_kernel(
-    wire, small, train, average, gains, send_a, recv_a, send_c, recv_c, rs, rr, cs, cr
+    wire, small, train, average, gains, mid,
+    send_a, recv_a, send_b, recv_b, send_c, recv_c, rs, rr, cs, cr,
 ):
     f = lax.axis_index("fsdp")
     t = lax.axis_index("tensor")
     sems = (rs, rr, cs, cr)
-    enter(f, t, lambda i: (2 * t + i // TENSOR, lax.rem(i, TENSOR)))
+    enter(f, t)
     small_first(f, t, small, gains, sems)
 
     def stage_a(n):
         j = lax.rem(f + n + 2 * t, FSDP)
-        k = lax.rem(f, 2) * TENSOR + t
-        is_own = (j == f) & (f // 2 == t)
-        return (wire.at[j], train.at[k], send_a.at[j], recv_a.at[k], (j, f // 2), is_own)
+        return (wire.at[j], mid.at[f], send_a.at[j], recv_a.at[f], (j, t), j == f)
+
+    def stage_b(n):
+        source = lax.rem(f - n - 2 * t + 2 * FSDP, FSDP)
+        to = source // 2
+        k = lax.rem(source, 2) * TENSOR + t
+        return source, (
+            mid.at[source], train.at[k], send_b.at[source], recv_b.at[k], (f, to), to == t,
+        )
 
     def stage_c(n):
-        k = lax.rem(n, 2) * TENSOR + lax.rem(n // 2 + f + t, TENSOR)
+        turn_at = lax.rem(f - n + FSDP, FSDP)
+        k = lax.rem(turn_at, 2) * TENSOR + lax.rem(turn_at // 2 - t + TENSOR, TENSOR)
         return k, (train.at[k], average.at[f], send_c.at[k], recv_c.at[f], (k, t), k == f)
 
     @pl.loop(0, FSDP)
     def _(n):
         send(*stage_a(n))
 
+    @pl.loop(0, FSDP)
+    def _(n):
+        source, copy = stage_b(n)
+        arrived(mid.at[source], recv_a.at[source])
+        send(*copy)
+
     small_second(f, t, small, gains, sems)
 
     @pl.loop(0, FSDP)
     def _(n):
         k, copy = stage_c(n)
-        arrived(train.at[k], recv_a.at[k])
+        arrived(train.at[k], recv_b.at[k])
         send(*copy)
 
     @pl.loop(0, FSDP)
@@ -236,6 +255,7 @@
     @pl.loop(0, FSDP)
     def _(n):
         sent(*stage_a(n))
+        sent(*stage_b(n)[1])
         sent(*stage_c(n)[1])
 
 
@@ -488,7 +508,7 @@
         [vmem] * 7 + [far] * 3,
         3,
     )
-    train, averages, gains = exchange(spread_kernel, out_wire, master_gains, 2, 0, 2, 1)
+    train, averages, gains = exchange(spread_kernel, out_wire, master_gains, 2, 1, 3, 1)
     train_turned, average_next = plain(
         finish_kernel,
         [jax.ShapeDtypeStruct((layers, block_cols, block_rows), jnp.bfloat16), flat],

time: 114 us -> 84.2 us (0.74)
  the two profiles are of different devices: /device:TPU:5 before, /device:TPU:6 now
where the time goes in v6:
time: 84.2 us; the launch traced here: 83.4 us
  Pallas kernels  81 us (96%)
  other arithmetic  0.95 us (1%)
    pallas_call x2, Pallas kernels, exchange(): pl.pallas_call(kernel, out_shape=[pieces] * outputs + [jax.ShapeDtypeStru...  62.2 us
    pallas_call x2, Pallas kernels, plain(): pl.pallas_call(kernel, out_shape=outputs, in_specs=specs, out_specs=out_s...  15.7 us
    pallas_call x1, Pallas kernels, on_device(): pl.pallas_call(prepare_kernel, out_shape=[wire_shape, one_row], in_specs=...  3.18 us

profile of v6, /device:TPU:6, one launch (start us, length us, event | category | flops | bytes accessed | tf_op | source)
XLA Modules:
  0.0 83.4 jit_solution(8078481561708293358)
XLA Ops:
  0.6 3.2 %shard_map.177 = (bf16[16,200,128]{2,1,0:T(8,128)(2,1)}, f32[1,128]{1,0:T(1,128)}) custom-call(bf16[2,96,2112]{2,1,0:T(8,128)(2,1)} %bitcast.19, bf16[2,24]{1,0:T(2,128)(2,1)} %gain_grads.1), custom_call_target="tpu_custom_call" | custom-call | tf_op jit(solution)/shard_map/pallas_call | solution.py:475
  3.8 25.4 %shard_map.178 = (bf16[16,200,128]{2,1,0:T(8,128)(2,1)}, f32[16,8,1,128]{3,2,1,0:T(1,128)}) custom-call(bf16[16,200,128]{2,1,0:T(8,128)(2,1)} %get-tuple-element.27.wire, f32[1,128]{1,0:T(1,128)} %get-tuple-element.28.small), custom_call_target="tpu_custom_call" | custom-call | tf_op jit(solution)/shard_map/pallas_call | solution.py:266
  29.3 8.9 %shard_map.179 = (bf16[16,200,128]{2,1,0:T(8,128)(2,1)}, f32[2,24]{1,0:T(2,128)}, f32[2,24]{1,0:T(2,128)}, f32[2,24]{1,0:T(2,128)}, f32[2,24]{1,0:T(2,128)}, /*i...) custom-call(bf16[16,200,128]{2,1,0:T(8,128)(2,1)} %get-tuple-element.29.pieces, ...), custom_call_target="tpu_custom_call" | custom-call | tf_op jit(solution)/shard_map/pallas_call | solution.py:439
  38.2 36.7 %shard_map.180 = (bf16[16,200,128]{2,1,0:T(8,128)(2,1)}, bf16[16,200,128]{2,1,0:T(8,128)(2,1)}, f32[16,8,2,24]{3,2,1,0:T(2,128)}) custom-call(bf16[16,200,128]{2,1,0:T(8,128)(2,1)} %get-tuple-element.31.wire, f32[2,24]{1,0:T(2,128)} %get-tuple-element.23.small), custom_call_target="tpu_custom_call" | custom-call | tf_op jit(solution)/shard_map/pallas_call | solution.py:266
  75.0 1.0 %convert_bitcast_fusion = bf16[2,16,8,24]{3,0,2,1:T(2,128)(2,1)S(1)} fusion(f32[16,8,2,24]{3,2,1,0:T(2,128)} %get-tuple-element.40), kind=kLoop, calls=%fused_computation | loop fusion | flops 6144 | bytes 36864 | tf_op jit(solution)/shard_map/transpose | solution.py:523
  75.9 0.7 reshape.27
  76.7 6.7 %shard_map.181 = (bf16[2,96,2112]{2,1,0:T(8,128)(2,1)}, f32[132,2,1536]{2,1,0:T(2,128)}) custom-call(bf16[16,200,128]{2,1,0:T(8,128)(2,1)} %get-tuple-element.33.train, bf16[16,200,128]{2,1,0:T(8,128)(2,1)} %get-tuple-element.34.pieces, f32[132,2,1536]{2,1,0:T(2,128)} %bitcast.18), custom_call_target="tpu_custom_call" | custom-call | tf_op jit(solution)/shard_map/pallas_call | solution.py:439
  (1 shorter events, 0.0 us)

commit v7 on v6

--- a/solution.py
+++ b/solution.py
@@ -24,6 +24,7 @@
 TENSOR = 8
 LANES = 128
 SPAN = 384
+LAG = 4
 
 
 def adam_step(gradient, master, first_state, second_state, clip_scale):
@@ -232,19 +233,21 @@
     def _(n):
         send(*stage_a(n))
 
-    @pl.loop(0, FSDP)
-    def _(n):
-        source, copy = stage_b(n)
-        arrived(mid.at[source], recv_a.at[source])
-        send(*copy)
-
     small_second(f, t, small, gains, sems)
 
-    @pl.loop(0, FSDP)
-    def _(n):
-        k, copy = stage_c(n)
-        arrived(train.at[k], recv_b.at[k])
-        send(*copy)
+    @pl.loop(0, FSDP + LAG)
+    def _(n):
+        @pl.when(n < FSDP)
+        def _():
+            source, copy = stage_b(n)
+            arrived(mid.at[source], recv_a.at[source])
+            send(*copy)
+
+        @pl.when(n >= LAG)
+        def _():
+            k, copy = stage_c(n - LAG)
+            arrived(train.at[k], recv_b.at[k])
+            send(*copy)
 
     @pl.loop(0, FSDP)
     def _(n):

time: 84.2 us -> 86.8 us (1.031)
  Pallas kernels: 81 us -> 82.9 us
    pallas_call x2, Pallas kernels: 62.2 us -> 64.1 us  [exchange(): pl.pallas_call(kernel, out_shape=[pieces] * outputs + [jax.ShapeDtypeStru...]
where the time goes in v7:
time: 86.8 us; the launch traced here: 85.3 us
  Pallas kernels  82.9 us (96%)
  other arithmetic  0.95 us (1%)
    pallas_call x2, Pallas kernels, exchange(): pl.pallas_call(kernel, out_shape=[pieces] * outputs + [jax.ShapeDtypeStru...  64.1 us
    pallas_call x2, Pallas kernels, plain(): pl.pallas_call(kernel, out_shape=outputs, in_specs=specs, out_specs=out_s...  15.7 us
    pallas_call x1, Pallas kernels, on_device(): pl.pallas_call(prepare_kernel, out_shape=[wire_shape, one_row], in_specs=...  3.18 us

profile of v7, /device:TPU:6, one launch (start us, length us, event | category | flops | bytes accessed | tf_op | source)
XLA Modules:
  0.0 85.3 jit_solution(17651715689031136663)
XLA Ops:
  0.6 3.2 %shard_map.177 = (bf16[16,200,128]{2,1,0:T(8,128)(2,1)}, f32[1,128]{1,0:T(1,128)}) custom-call(bf16[2,96,2112]{2,1,0:T(8,128)(2,1)} %bitcast.19, bf16[2,24]{1,0:T(2,128)(2,1)} %gain_grads.1), custom_call_target="tpu_custom_call" | custom-call | tf_op jit(solution)/shard_map/pallas_call | solution.py:478
  3.8 25.4 %shard_map.178 = (bf16[16,200,128]{2,1,0:T(8,128)(2,1)}, f32[16,8,1,128]{3,2,1,0:T(1,128)}) custom-call(bf16[16,200,128]{2,1,0:T(8,128)(2,1)} %get-tuple-element.27.wire, f32[1,128]{1,0:T(1,128)} %get-tuple-element.28.small), custom_call_target="tpu_custom_call" | custom-call | tf_op jit(solution)/shard_map/pallas_call | solution.py:269
  29.3 8.9 %shard_map.179 = (bf16[16,200,128]{2,1,0:T(8,128)(2,1)}, f32[2,24]{1,0:T(2,128)}, f32[2,24]{1,0:T(2,128)}, f32[2,24]{1,0:T(2,128)}, f32[2,24]{1,0:T(2,128)}, /*i...) custom-call(bf16[16,200,128]{2,1,0:T(8,128)(2,1)} %get-tuple-element.29.pieces, ...), custom_call_target="tpu_custom_call" | custom-call | tf_op jit(solution)/shard_map/pallas_call | solution.py:442
  38.2 38.6 %shard_map.180 = (bf16[16,200,128]{2,1,0:T(8,128)(2,1)}, bf16[16,200,128]{2,1,0:T(8,128)(2,1)}, f32[16,8,2,24]{3,2,1,0:T(2,128)}) custom-call(bf16[16,200,128]{2,1,0:T(8,128)(2,1)} %get-tuple-element.31.wire, f32[2,24]{1,0:T(2,128)} %get-tuple-element.23.small), custom_call_target="tpu_custom_call" | custom-call | tf_op jit(solution)/shard_map/pallas_call | solution.py:269
  76.9 1.0 %convert_bitcast_fusion = bf16[2,16,8,24]{3,0,2,1:T(2,128)(2,1)S(1)} fusion(f32[16,8,2,24]{3,2,1,0:T(2,128)} %get-tuple-element.40), kind=kLoop, calls=%fused_computation | loop fusion | flops 6144 | bytes 36864 | tf_op jit(solution)/shard_map/transpose | solution.py:526
  77.8 0.7 reshape.27
  78.6 6.8 %shard_map.181 = (bf16[2,96,2112]{2,1,0:T(8,128)(2,1)}, f32[132,2,1536]{2,1,0:T(2,128)}) custom-call(bf16[16,200,128]{2,1,0:T(8,128)(2,1)} %get-tuple-element.33.train, bf16[16,200,128]{2,1,0:T(8,128)(2,1)} %get-tuple-element.34.pieces, f32[132,2,1536]{2,1,0:T(2,128)} %bitcast.18), custom_call_target="tpu_custom_call" | custom-call | tf_op jit(solution)/shard_map/pallas_call | solution.py:442
  (1 shorter events, 0.0 us)
